TPU v7x, 128 devices: a whole 4x4x4 slice. The times are simulated.
128 devices in a mesh: wide: 16 (over z_hi, y, core), narrow: 8 (over x, z_lo).
Axes of the slice: x: 4, y: 4, z: 4 (z_hi: 2, z_lo: 2; z = z_hi * 2 + z_lo), core: 2. Of those that a mesh axis runs over, the one named last changes fastest.
Arguments:
- field: float32 [4, 512, 512, 256], P(None, 'wide', 'narrow'), may hold values from -70 to 70, as said below
- start_first: float32 [512, 128], replicated, may hold values from -5 to 5
- start_second: float32 [512, 128], replicated, may hold values from -5 to 5
Outputs:
- core_tensor: float32 [256, 4, 128, 128], P('wide', None, 'narrow')
- basis_first: float32 [512, 128], replicated
- basis_second: float32 [512, 128], replicated
Inputs may be any that keep to these rules, and one draw needn't show every extreme that they name: `field`: species fields with amplitudes that vary over mode 1, mode 2 and mode 3.
All inputs are finite; a program needn't handle non-finite values.
Results may differ from a plain program's by a relative error of at most 0.0003.
Values sent between devices are 32-bit elements; how exact they have to be, the bound alone decides.
No kernel may reach another device: no remote copies, remote signals or barrier semaphores. Data moves between devices by JAX's collectives and lax.ppermute only.
A program may use at most 192 MiB of HBM per device.

v0:
```python
import functools
import jax
import jax.numpy as jnp
from jax import lax
from jax.experimental import pallas as pl
from jax.experimental.pallas import tpu as pltpu
from jax.sharding import Mesh, PartitionSpec as P

ITERS = 3
F32 = jnp.float32
BF16 = jnp.bfloat16
EXACT = lax.Precision.HIGHEST
ALL = ("board", "core", "narrow")
CHIPS = ("board", "narrow")
SWAP = [(0, 1), (1, 0)]
MIB = 1024 * 1024

NN = (((1,), (0,)), ((), ()))
NT = (((1,), (1,)), ((), ()))
TN = (((0,), (0,)), ((), ()))


def dot32(a, b, dims):
    return lax.dot_general(a, b, dims, precision=EXACT, preferred_element_type=F32)


def dot16(a, b, dims):
    return lax.dot_general(a, b, dims, preferred_element_type=F32)


def split2(x):
    high = x.astype(BF16)
    low = (x - high.astype(F32)).astype(BF16)
    return high, low


def split3(x):
    high = x.astype(BF16)
    rest = x - high.astype(F32)
    mid = rest.astype(BF16)
    low = (rest - mid.astype(F32)).astype(BF16)
    return high, mid, low


def planes_kernel(me_ref, core_ref, x_ref, out_ref):
    ib = x_ref.shape[1]
    rows = x_ref.shape[3]
    flat = out_ref.reshape(rows * ib, out_ref.shape[2])
    for i in range(ib):
        pair = jnp.concatenate([x_ref[0, i], x_ref[1, i]], axis=0)
        flat[pl.ds(i, rows, stride=ib), :] = pair.T


def planes_first(me, core, field):
    species, cells, points, planes = field.shape
    ib = 8
    blocks = cells // ib
    return pl.pallas_call(
        planes_kernel,
        grid=(species // 2, blocks),
        in_specs=[pl.BlockSpec(memory_space=pltpu.SMEM)] * 2
        + [pl.BlockSpec((2, ib, points, planes), lambda c, g: (c, g, 0, 0))],
        out_specs=pl.BlockSpec((planes, ib, 2 * points), lambda c, g: (0, c * blocks + g, 0)),
        out_shape=jax.ShapeDtypeStruct((planes, cells * species // 2, 2 * points), F32),
        compiler_params=pltpu.CompilerParams(vmem_limit_bytes=60 * MIB),
        name="planes_first",
    )(me, core, field)


def lower_blocks(n):
    return [(r, c) for r in range(n) for c in range(r + 1)]


def store_lower(core_ref, keep_ref, send_ref, packed, main, cross):
    n = main.shape[0] // 128
    for b, (r, c) in enumerate(lower_blocks(n)):
        rs, cs = slice(128 * r, 128 * r + 128), slice(128 * c, 128 * c + 128)
        packed[128 * b : 128 * b + 128, :] = main[rs, cs] + cross[rs, cs] + cross[cs, rs].T
    half = keep_ref.shape[0]
    keep_ref[...] = packed[pl.ds(pl.multiple_of(core_ref[0] * half, half), half), :]
    send_ref[...] = packed[pl.ds(pl.multiple_of((1 - core_ref[0]) * half, half), half), :]


def gram_first_kernel(steps, core_ref, y_ref, keep_ref, send_ref, packed, main, cross):
    step = pl.program_id(0)
    size = main.shape[0]
    parts = [
        y_ref[:, n, tau, c].reshape(size, 128)
        for n in range(y_ref.shape[1])
        for tau in range(2)
        for c in range(2)
    ]
    high, low = split2(jnp.concatenate(parts, axis=1))
    mixed = dot16(high, low, NT)
    full = dot16(high, high, NT)

    @pl.when(step == 0)
    def _():
        main[...] = full
        cross[...] = mixed

    @pl.when(step > 0)
    def _():
        main[...] += full
        cross[...] += mixed

    @pl.when(step == steps - 1)
    def _():
        store_lower(core_ref, keep_ref, send_ref, packed, main, cross)


GRAM_POINTS = 2


def gram_first(core, y):
    wide, narrow, _, groups, cells, lanes = y.shape
    size = wide * cells
    count = size // 128
    rows = 128 * (count * (count + 1) // 2)
    steps = narrow // GRAM_POINTS
    return pl.pallas_call(
        functools.partial(gram_first_kernel, steps),
        grid=(steps,),
        in_specs=[
            pl.BlockSpec(memory_space=pltpu.SMEM),
            pl.BlockSpec(
                (wide, GRAM_POINTS, 2, groups, cells, lanes), lambda g: (0, g, 0, 0, 0, 0)
            ),
        ],
        out_specs=[pl.BlockSpec((rows // 2, 128), lambda g: (0, 0))] * 2,
        out_shape=[jax.ShapeDtypeStruct((rows // 2, 128), F32)] * 2,
        scratch_shapes=[
            pltpu.VMEM((rows, 128), F32),
            pltpu.VMEM((size, size), F32),
            pltpu.VMEM((size, size), F32),
        ],
        compiler_params=pltpu.CompilerParams(vmem_limit_bytes=50 * MIB),
        name="gram_first",
    )(core, y)


def summed_pieces(keep, send, chips):
    half = keep + lax.ppermute(send, "core", SWAP)
    pieces = half.reshape(chips, 1, half.shape[0] * 128 // chips)
    return jnp.sum(lax.all_to_all(pieces, CHIPS, 0, 0, tiled=True), axis=0)


def gathered_half(own, chips):
    copies = jnp.broadcast_to(own[None], (chips, *own.shape))
    return lax.all_to_all(copies, CHIPS, 0, 0, tiled=True).reshape(-1, 128)


def swapped(mine):
    return lax.ppermute(mine, "core", SWAP)


WINDOW, PANEL = 32, 16


def inverse_factor(gram):
    size = gram.shape[0]
    row = lax.broadcasted_iota(jnp.int32, (size, size), 0)
    col = lax.broadcasted_iota(jnp.int32, (size, size), 1)
    work = jnp.concatenate([gram, jnp.where(row == col, 1.0, 0.0).astype(F32)], axis=1)
    low = lax.broadcasted_iota(jnp.int32, (8, size), 0)
    blocks = WINDOW // 8

    def spread(x):
        return jnp.broadcast_to(x, (8, x.shape[1]))

    done, scales = [], []
    for base in range(0, size, WINDOW):
        rows = [work[8 * i : 8 * i + 8] for i in range(blocks)]
        inverses, pivots = [None] * blocks, [None] * blocks
        for first in range(0, WINDOW, PANEL):
            cols = {}
            for j in range(PANEL):
                c = base + first + j
                for i in range(first // 8, blocks):
                    cols[j, i] = jnp.broadcast_to(rows[i][:, c : c + 1], (8, size))
            for k in range(PANEL):
                here, at = (first + k) // 8, k % 8
                pivot = spread(cols[k, here][at : at + 1])
                inverse = 1.0 / pivot
                ratio = {i: cols[k, i] * inverse for i in range(here, blocks)}
                ratio[here] = jnp.where(low > at, ratio[here], 0.0)
                for j in range(k + 1, PANEL):
                    piece = spread(cols[j, here][at : at + 1])
                    for i in range(here, blocks):
                        cols[j, i] = cols[j, i] - ratio[i] * piece
                piece = spread(rows[here][at : at + 1])
                for i in range(here, blocks):
                    rows[i] = rows[i] - jnp.concatenate([ratio[i], ratio[i]], axis=1) * piece
                inverses[here] = jnp.where(low == at, inverse, inverses[here]) if at else inverse
                pivots[here] = jnp.where(low == at, pivot, pivots[here]) if at else pivot
        done += [r[:, size:] for r in rows]
        scales += pivots
        if base + WINDOW < size:
            left = [r[:, :size] * s for r, s in zip(rows, inverses)]
            lh, lm, ll = split3(jnp.concatenate(left, axis=0))
            rh, rm, rl = split3(jnp.concatenate(rows, axis=0))
            lhs = jnp.concatenate([lh, lh, lh, lm, lm, ll], axis=0)
            rhs = jnp.concatenate([rh, rm, rl, rh, rm, rh], axis=0)
            work = work[WINDOW:] - dot16(lhs, rhs, TN)[base + WINDOW :]
    return jnp.concatenate([d * (1.0 / jnp.sqrt(p)) for d, p in zip(done, scales)], axis=0)


def orthonormal_rows(rows):
    rank = rows.shape[0]
    h, m, l = split3(rows)
    stack = jnp.concatenate([h, m, l], axis=0)
    d = dot16(stack, stack, NT)
    a, b = slice(0, rank), slice(rank, 2 * rank)
    c = slice(2 * rank, 3 * rank)
    gram = d[a, a] + (d[a, b] + d[b, a]) + (d[b, b] + (d[a, c] + d[c, a]))
    th, tm, tl = split3(inverse_factor(gram))
    return dot16(
        jnp.concatenate([th, th, th, tm, tm, tl], axis=1),
        jnp.concatenate([h, m, l, h, m, h], axis=0),
        NN,
    )


def start_kernel(start_ref, out_ref):
    out_ref[...] = orthonormal_rows(start_ref[...].T)


def start_rows(start):
    return pl.pallas_call(
        start_kernel,
        out_shape=jax.ShapeDtypeStruct(start.shape[::-1], F32),
        compiler_params=pltpu.CompilerParams(vmem_limit_bytes=8 * MIB),
        name="start_rows",
    )(start)


def basis_kernel(core_ref, mine_ref, other_ref, start_ref, rows_ref, basis_ref, packed, gram):
    half = mine_ref.shape[0]
    packed[pl.ds(pl.multiple_of(core_ref[0] * half, half), half), :] = mine_ref[...]
    packed[pl.ds(pl.multiple_of((1 - core_ref[0]) * half, half), half), :] = other_ref[...]
    n = gram.shape[0] // 128
    for b, (r, c) in enumerate(lower_blocks(n)):
        rs, cs = slice(128 * r, 128 * r + 128), slice(128 * c, 128 * c + 128)
        block = packed[128 * b : 128 * b + 128, :]
        gram[rs, cs] = block
        if r != c:
            gram[cs, rs] = block.T

    def sweep(_, rows):
        return orthonormal_rows(dot32(rows, gram[...], NN))

    rows = lax.fori_loop(0, ITERS, sweep, start_ref[...])
    rows_ref[...] = rows
    basis_ref[...] = rows.T


def basis_rows(core, mine, other, start):
    rank, size = start.shape
    whole = pl.BlockSpec(memory_space=pltpu.VMEM)
    return pl.pallas_call(
        basis_kernel,
        in_specs=[pl.BlockSpec(memory_space=pltpu.SMEM), whole, whole, whole],
        out_shape=(
            jax.ShapeDtypeStruct((rank, size), F32),
            jax.ShapeDtypeStruct((size, rank), F32),
        ),
        scratch_shapes=[
            pltpu.VMEM((2 * mine.shape[0], 128), F32),
            pltpu.VMEM((size, size), F32),
        ],
        compiler_params=pltpu.CompilerParams(vmem_limit_bytes=16 * MIB),
        name="basis_rows",
    )(core, mine, other, start)


def reduce_kernel(me_ref, core_ref, rows_ref, y_ref, *refs):
    *out_refs, keep_ref, send_ref, packed, reduced, main, cross = refs
    step = pl.program_id(0)
    rank, size = rows_ref.shape
    narrow = len(out_refs)
    per = rank // narrow
    bh, bl = split2(rows_ref[...])
    both = jnp.concatenate([bh, bl], axis=0)
    lane = lax.broadcasted_iota(jnp.int32, (rank, 128), 1)
    for m in range(narrow // 2):
        parts = [y_ref[:, 2 * m + h, 0, 0].reshape(size, 128) for h in range(2)]
        yh, yl = split2(jnp.concatenate(parts, axis=1))
        wide = dot16(both, yh, NN)
        got = wide[:rank] + (wide[rank:] + dot16(bh, yl, NN))
        a, b = got[:, :128], got[:, 128:]
        lanes = slice(128 * m, 128 * m + 128)
        reduced[:rank, lanes] = jnp.where(lane < 64, a, pltpu.roll(b, 64, 1))
        reduced[rank:, lanes] = jnp.where(lane < 64, pltpu.roll(a, 64, 1), b)
    for j, out_ref in enumerate(out_refs):
        owner = lax.rem(me_ref[0] + j, narrow)
        for s in range(2):
            start = pl.multiple_of(rank * s + owner * per, per)
            out_ref[0, s] = reduced[pl.ds(start, per), :]
    high, low = split2(reduced[...])
    full = dot16(high, high, TN)
    mixed = dot16(high, low, TN)

    @pl.when(step == 0)
    def _():
        main[...] = full
        cross[...] = mixed

    @pl.when(step > 0)
    def _():
        main[...] += full
        cross[...] += mixed

    @pl.when(step == 3)
    def _():
        store_lower(core_ref, keep_ref, send_ref, packed, main, cross)


def reduce_first(me, core, rows, y):
    wide, narrow, _, groups, cells, lanes = y.shape
    rank, size = rows.shape
    points = narrow * 64
    count = points // 128
    packed = 128 * (count * (count + 1) // 2)
    per = rank // narrow
    *blocks, keep, send = pl.pallas_call(
        reduce_kernel,
        grid=(2 * groups,),
        in_specs=[
            pl.BlockSpec(memory_space=pltpu.SMEM),
            pl.BlockSpec(memory_space=pltpu.SMEM),
            pl.BlockSpec((rank, size), lambda g: (0, 0)),
            pl.BlockSpec((wide, narrow, 1, 1, cells, lanes), lambda g: (0, 0, g % 2, g // 2, 0, 0)),
        ],
        out_specs=[pl.BlockSpec((1, 2, per, points), lambda g: (g, 0, 0, 0))] * narrow
        + [pl.BlockSpec((packed // 2, 128), lambda g: (0, 0))] * 2,
        out_shape=[jax.ShapeDtypeStruct((2 * groups, 2, per, points), F32)] * narrow
        + [jax.ShapeDtypeStruct((packed // 2, 128), F32)] * 2,
        scratch_shapes=[
            pltpu.VMEM((packed, 128), F32),
            pltpu.VMEM((2 * rank, points), F32),
            pltpu.VMEM((points, points), F32),
            pltpu.VMEM((points, points), F32),
        ],
        compiler_params=pltpu.CompilerParams(vmem_limit_bytes=48 * MIB),
        name="reduce_first",
    )(me, core, rows, y)
    return blocks, keep, send


def core_kernel(me_ref, rows_ref, *refs):
    *block_refs, out_ref = refs
    narrow = len(block_refs)
    taus, lows, per, points = block_refs[0].shape
    rank = rows_ref.shape[0]
    count = taus * lows * per
    bh, bl = split2(rows_ref[...])
    both = jnp.concatenate([bh, bl], axis=0)
    rows = jnp.concatenate([r[...].reshape(count, points) for r in block_refs], axis=0)
    rh, rl = split2(rows)
    wide = dot16(rh, both, NT)
    got = wide[:, :rank] + (wide[:, rank:] + dot16(rl, bh, NT))
    for j in range(narrow):
        source = lax.rem(me_ref[0] + (narrow - j), narrow)
        block = got[count * j : count * (j + 1)].reshape(taus, lows, per, rank)
        for tau in range(taus):
            out_ref[taus * source + tau] = block[tau]


def core_blocks(me, rows, blocks):
    rank, points = rows.shape
    narrow = len(blocks)
    steps, lows, per, _ = blocks[0].shape
    groups = steps // 2
    return pl.pallas_call(
        core_kernel,
        grid=(groups,),
        in_specs=[
            pl.BlockSpec(memory_space=pltpu.SMEM),
            pl.BlockSpec((rank, points), lambda g: (0, 0)),
        ]
        + [pl.BlockSpec((2, lows, per, points), lambda g: (g, 0, 0, 0))] * narrow,
        out_specs=pl.BlockSpec((2 * narrow, lows, per, rank), lambda g: (0, g, 0, 0)),
        out_shape=jax.ShapeDtypeStruct((2 * narrow, groups * lows, per, rank), F32),
        compiler_params=pltpu.CompilerParams(vmem_limit_bytes=12 * MIB),
        name="core_blocks",
    )(me, rows, *blocks)


def whole(field, start_first, start_second):
    narrow = lax.axis_size("narrow")
    wide = lax.axis_size("board") * lax.axis_size("core")
    chips = lax.axis_size("board") * narrow
    me = lax.axis_index("narrow").astype(jnp.int32).reshape(1)
    core = lax.axis_index("core").astype(jnp.int32).reshape(1)
    planes = lax.all_to_all(planes_first(me, core, field), ALL, 0, 0, tiled=True)
    y = planes.reshape(wide, narrow, 2, field.shape[0] // 2, field.shape[1], planes.shape[2])
    rows_first = start_rows(start_first)
    rows_second = start_rows(start_second)
    own = summed_pieces(*gram_first(core, y), chips)
    mine = gathered_half(own, chips)
    rows_first, basis_first = basis_rows(core, mine, swapped(mine), rows_first)
    blocks, keep, send = reduce_first(me, core, rows_first, y)
    own, blocks = lax.optimization_barrier((summed_pieces(keep, send, chips), blocks))
    moved = [
        lax.ppermute(blocks[j], "narrow", [(n, (n + j) % narrow) for n in range(narrow)])
        for j in range(1, narrow)
    ]
    mine = gathered_half(own, chips)
    rows_second, basis_second = basis_rows(core, mine, swapped(mine), rows_second)
    return (core_blocks(me, rows_second, [blocks[0]] + moved), basis_first, basis_second)


def solution(mesh):
    wide, narrow = mesh.devices.shape
    finer = Mesh(mesh.devices.reshape(wide // 2, 2, narrow), ALL)
    first = ("board", "core")
    return jax.shard_map(
        whole,
        mesh=finer,
        in_specs=(P(None, first, "narrow", None), P(), P()),
        out_specs=(P(first, None, "narrow", None), P(), P()),
        check_vma=False,
    )
```

profile of v0, /device:TPU:1, one launch (start us, length us, event | category | flops | bytes accessed | tf_op | source)
XLA Modules:
  0.0 267.2 jit_solution(1337255590319555350)
XLA Ops:
  0.6 10.1 %planes_first.1 = f32[256,64,128]{2,1,0:T(8,128)} custom-call(s32[1]{0:T(128)} %bitcast.me_ref, s32[1]{0:T(128)} %bitcast.1.core_ref, f32[4,32,64,256]{3,2,1,0:T(8,128)} %x_ref.1), custom_call_target="tpu_custom_call" | custom-call | tf_op jit(solution)/shard_map/planes_first/pallas_call | solution.py:58
  10.7 107.3 %all_to_all.25 = f32[256,64,128]{2,1,0:T(8,128)} all-to-all(f32[256,64,128]{2,1,0:T(8,128)} %planes_first.1), channel_id=1, replica_groups=mesh['board'=8,'core'=2,'narrow'=8] {'board','core','narrow'}, dimensions={0} | all-to-all | bytes 16777216 | tf_op jit(solution)/shard_map/all_to_all | solution.py:395
  118.0 0.0 copy-start
  118.0 8.0 %gram_first.1 = (f32[640,128]{1,0:T(8,128)S(1)}, f32[640,128]{1,0:T(8,128)S(1)}) custom-call(s32[1]{0:T(128)} %bitcast.1.core_ref, f32[16,8,2,2,32,128]{5,4,3,2,1,0:T(8,128)} %bitcast.11), custom_call_target="tpu_custom_call" | custom-call | tf_op jit(solution)/shard_map/gram_first/pallas_call | solution.py:121
  126.0 0.0 copy-start.1
  126.0 2.7 %collective-permute-start = (f32[640,128]{1,0:T(8,128)S(1)}, f32[640,128]{1,0:T(8,128)S(1)}, u32[]{:S(2)}, u32[]{:S(2)}) collective-permute-start(f32[640,128]{1,0:T(8,128)S(1)} %get-tuple-element.29), channel_id=1, source_target_pairs={{0,8},{8,0},{1,9},{9,1},{2,10},{10,2},{3,11},{11,3},{4,12},{12,4},... | collective-permute-start | bytes 983048 | tf_op jit(solution)/shard_map/ppermute | solution.py:143
  128.7 1.3 collective-permute-done
  130.0 15.7 %all_to_all.26 = f32[64,1,1280]{2,1,0:T(1,128)S(1)} all-to-all(f32[64,1,1280]{2,1,0:T(1,128)S(1)} %bitcast.13), channel_id=1, replica_groups=mesh['board'=8,'core'=2,'narrow'=8] {'board','narrow'}, dimensions={0} | all-to-all | bytes 655360 | tf_op jit(solution)/shard_map/all_to_all | solution.py:145
  145.6 0.2 reduce_sum.20
  145.8 0.2 broadcast_in_dim.6
  146.0 14.6 %all_to_all.27 = f32[64,1,1280]{2,1,0:T(1,128)S(1)} all-to-all(f32[64,1,1280]{2,1,0:T(1,128)S(1)} %broadcast_in_dim.6), channel_id=1, replica_groups=mesh['board'=8,'core'=2,'narrow'=8] {'board','narrow'}, dimensions={0} | all-to-all | bytes 655360 | tf_op jit(solution)/shard_map/all_to_all | solution.py:150
  160.6 3.2 %collective-permute-start.1 = (f32[640,128]{1,0:T(8,128)S(1)}, f32[640,128]{1,0:T(8,128)S(1)}, u32[]{:S(2)}, u32[]{:S(2)}) collective-permute-start(f32[640,128]{1,0:T(8,128)S(1)} %bitcast.9), channel_id=1, source_target_pairs={{0,8},{8,0},{1,9},{9,1},{2,10},{10,2},{3,11},{11,3},{4,12},{12,4},... | collective-permute-start | bytes 983048 | tf_op jit(solution)/shard_map/ppermute | solution.py:154
  163.8 0.0 copy-done
  163.8 3.9 %start_rows.2.start_ref = f32[128,512]{1,0:T(8,128)S(1)} custom-call(f32[512,128]{1,0:T(8,128)S(1)} %copy-done), custom_call_target="tpu_custom_call" | custom-call | tf_op jit(solution)/shard_map/start_rows/pallas_call | solution.py:229
  167.7 0.0 collective-permute-done.1.other_ref
  167.7 14.4 %basis_rows.2 = (f32[128,512]{1,0:T(8,128)S(1)}, f32[512,128]{1,0:T(8,128)}) custom-call(s32[1]{0:T(128)} %bitcast.1.core_ref, f32[640,128]{1,0:T(8,128)S(1)} %bitcast.10, f32[640,128]{1,0:T(8,128)S(1)} %collective-permute-done.1.other_ref, f32[128,512]{1,0:T(8,128)S(1)} %start_rows.2.start_ref), custom_call_target="tpu_custom_call" | custom-call | tf_op jit(solution)/shard_map/basis_rows/pallas_call | solution.py:260
  182.1 7.5 %reduce_first.1 = (f32[4,2,16,512]{3,2,1,0:T(8,128)S(1)}, f32[4,2,16,512]{3,2,1,0:T(8,128)S(1)}, f32[4,2,16,512]{3,2,1,0:T(8,128)S(1)}, f32[4,2,16,512]{3,2,1,0:...) custom-call(s32[1]{0:T(128)} %bitcast.me_ref, ...), custom_call_target="tpu_custom_call" | custom-call | tf_op jit(solution)/shard_map/reduce_first/pallas_call | solution.py:325
  189.6 0.1 collective-permute-start.2
  189.7 1.6 collective-permute-done.2
  191.3 15.1 %all_to_all.28 = f32[64,1,1280]{2,1,0:T(1,128)S(1)} all-to-all(f32[64,1,1280]{2,1,0:T(1,128)S(1)} %bitcast.14), channel_id=1, replica_groups=mesh['board'=8,'core'=2,'narrow'=8] {'board','narrow'}, dimensions={0} | all-to-all | bytes 655360 | tf_op jit(solution)/shard_map/all_to_all | solution.py:145
  206.4 0.2 reduce_sum.21
  206.7 0.2 broadcast_in_dim.16
  206.8 14.4 %all_to_all.29 = f32[64,1,1280]{2,1,0:T(1,128)S(1)} all-to-all(f32[64,1,1280]{2,1,0:T(1,128)S(1)} %broadcast_in_dim.16), channel_id=1, replica_groups=mesh['board'=8,'core'=2,'narrow'=8] {'board','narrow'}, dimensions={0} | all-to-all | bytes 655360 | tf_op jit(solution)/shard_map/all_to_all | solution.py:150
  221.2 2.9 %collective-permute-start.3 = (f32[640,128]{1,0:T(8,128)S(1)}, f32[640,128]{1,0:T(8,128)S(1)}, u32[]{:S(2)}, u32[]{:S(2)}) collective-permute-start(f32[640,128]{1,0:T(8,128)S(1)} %bitcast.7), channel_id=1, source_target_pairs={{0,8},{8,0},{1,9},{9,1},{2,10},{10,2},{3,11},{11,3},{4,12},{12,4},... | collective-permute-start | bytes 983048 | tf_op jit(solution)/shard_map/ppermute | solution.py:154
  224.1 0.7 collective-permute-start.10
  224.8 0.8 collective-permute-start.4
  225.6 0.3 collective-permute-start.5
  225.9 1.4 collective-permute-start.6
  227.3 10.3 %collective-permute-done.10.refs_7_ = f32[4,2,16,512]{3,2,1,0:T(8,128)S(1)} collective-permute-done((f32[4,2,16,512]{3,2,1,0:T(8,128)S(1)}, f32[4,2,16,512]{3,2,1,0:T(8,128)S(1)}, u32[]{:S(2)}, u32[]{:S(2)}) %collective-permute-start.10) | collective-permute-done | bytes 262176 | tf_op jit(solution)/shard_map/ppermute | solution.py:405
  237.6 1.2 collective-permute-start.7
  238.8 3.8 %collective-permute-done.4.refs_1_ = f32[4,2,16,512]{3,2,1,0:T(8,128)S(1)} collective-permute-done((f32[4,2,16,512]{3,2,1,0:T(8,128)S(1)}, f32[4,2,16,512]{3,2,1,0:T(8,128)S(1)}, u32[]{:S(2)}, u32[]{:S(2)}) %collective-permute-start.4) | collective-permute-done | bytes 262176 | tf_op jit(solution)/shard_map/ppermute | solution.py:405
  242.5 3.1 %collective-permute-start.8 = (f32[4,2,16,512]{3,2,1,0:T(8,128)S(1)}, f32[4,2,16,512]{3,2,1,0:T(8,128)S(1)}, u32[]{:S(2)}, u32[]{:S(2)}) collective-permute-start(f32[4,2,16,512]{3,2,1,0:T(8,128)S(1)} %get-tuple-element.48), channel_id=1, source_target_pairs={{0,5},{1,6},{2,7},{3,0},{4,1},{5,2},{6,3},{7,4},{8,13},{9,14},{10,... | collective-permute-start | bytes 786440 | tf_op jit(solution)/shard_map/ppermute | solution.py:405
  245.6 0.0 collective-permute-done.3.other_ref
  245.6 1.6 collective-permute-start.9
  247.2 0.0 copy-done.1
  247.2 3.9 %start_rows.3.start_ref = f32[128,512]{1,0:T(8,128)S(1)} custom-call(f32[512,128]{1,0:T(8,128)S(1)} %copy-done.1), custom_call_target="tpu_custom_call" | custom-call | tf_op jit(solution)/shard_map/start_rows/pallas_call | solution.py:229
  251.1 14.4 %basis_rows.3 = (f32[128,512]{1,0:T(8,128)S(1)}, f32[512,128]{1,0:T(8,128)}) custom-call(s32[1]{0:T(128)} %bitcast.1.core_ref, f32[640,128]{1,0:T(8,128)S(1)} %bitcast.8, f32[640,128]{1,0:T(8,128)S(1)} %collective-permute-done.3.other_ref, f32[128,512]{1,0:T(8,128)S(1)} %start_rows.3.start_ref), custom_call_target="tpu_custom_call" | custom-call | tf_op jit(solution)/shard_map/basis_rows/pallas_call | solution.py:260
  265.4 0.0 collective-permute-done.5.refs_2_
  265.5 0.0 collective-permute-done.6.refs_3_
  265.5 0.0 collective-permute-done.7.refs_4_
  265.5 0.0 collective-permute-done.8.refs_5_
  265.5 0.0 collective-permute-done.9.refs_6_
  265.5 1.7 core_blocks.1
  (4 shorter events, 0.1 us)
Async XLA Ops:
  118.0 45.8 %copy-start = (f32[512,128]{1,0:T(8,128)S(1)}, f32[512,128]{1,0:T(8,128)}, u32[]{:S(2)}) copy-start(f32[512,128]{1,0:T(8,128)} %start_ref.2) | copy-start | bytes 786436
  126.0 121.2 %copy-start.1 = (f32[512,128]{1,0:T(8,128)S(1)}, f32[512,128]{1,0:T(8,128)}, u32[]{:S(2)}) copy-start(f32[512,128]{1,0:T(8,128)} %start_ref.3) | copy-start | bytes 786436
  126.0 3.9 %collective-permute-start = (f32[640,128]{1,0:T(8,128)S(1)}, f32[640,128]{1,0:T(8,128)S(1)}, u32[]{:S(2)}, u32[]{:S(2)}) collective-permute-start(f32[640,128]{1,0:T(8,128)S(1)} %get-tuple-element.29), channel_id=1, source_target_pairs={{0,8},{8,0},{1,9},{9,1},{2,10},{10,2},{3,11},{11,3},{4,12},{12,4},... | collective-permute-start | bytes 983048 | tf_op jit(solution)/shard_map/ppermute | solution.py:143
  160.6 7.1 %collective-permute-start.1 = (f32[640,128]{1,0:T(8,128)S(1)}, f32[640,128]{1,0:T(8,128)S(1)}, u32[]{:S(2)}, u32[]{:S(2)}) collective-permute-start(f32[640,128]{1,0:T(8,128)S(1)} %bitcast.9), channel_id=1, source_target_pairs={{0,8},{8,0},{1,9},{9,1},{2,10},{10,2},{3,11},{11,3},{4,12},{12,4},... | collective-permute-start | bytes 983048 | tf_op jit(solution)/shard_map/ppermute | solution.py:154
  189.6 1.7 collective-permute-start.2
  221.2 24.4 %collective-permute-start.3 = (f32[640,128]{1,0:T(8,128)S(1)}, f32[640,128]{1,0:T(8,128)S(1)}, u32[]{:S(2)}, u32[]{:S(2)}) collective-permute-start(f32[640,128]{1,0:T(8,128)S(1)} %bitcast.7), channel_id=1, source_target_pairs={{0,8},{8,0},{1,9},{9,1},{2,10},{10,2},{3,11},{11,3},{4,12},{12,4},... | collective-permute-start | bytes 983048 | tf_op jit(solution)/shard_map/ppermute | solution.py:154
  224.1 13.5 %collective-permute-start.10 = (f32[4,2,16,512]{3,2,1,0:T(8,128)S(1)}, f32[4,2,16,512]{3,2,1,0:T(8,128)S(1)}, u32[]{:S(2)}, u32[]{:S(2)}) collective-permute-start(f32[4,2,16,512]{3,2,1,0:T(8,128)S(1)} %get-tuple-element.50), channel_id=1, source_target_pairs={{0,7},{1,0},{2,1},{3,2},{4,3},{5,4},{6,5},{7,6},{8,15},{9,8},{10,9... | collective-permute-start | bytes 786440 | tf_op jit(solution)/shard_map/ppermute | solution.py:405
  224.8 17.7 %collective-permute-start.4 = (f32[4,2,16,512]{3,2,1,0:T(8,128)S(1)}, f32[4,2,16,512]{3,2,1,0:T(8,128)S(1)}, u32[]{:S(2)}, u32[]{:S(2)}) collective-permute-start(f32[4,2,16,512]{3,2,1,0:T(8,128)S(1)} %get-tuple-element.44), channel_id=1, source_target_pairs={{0,1},{1,2},{2,3},{3,4},{4,5},{5,6},{6,7},{7,0},{8,9},{9,10},{10,1... | collective-permute-start | bytes 786440 | tf_op jit(solution)/shard_map/ppermute | solution.py:405
  225.6 39.9 %collective-permute-start.5 = (f32[4,2,16,512]{3,2,1,0:T(8,128)S(1)}, f32[4,2,16,512]{3,2,1,0:T(8,128)S(1)}, u32[]{:S(2)}, u32[]{:S(2)}) collective-permute-start(f32[4,2,16,512]{3,2,1,0:T(8,128)S(1)} %get-tuple-element.45), channel_id=1, source_target_pairs={{0,2},{1,3},{2,4},{3,5},{4,6},{5,7},{6,0},{7,1},{8,10},{9,11},{10,... | collective-permute-start | bytes 786440 | tf_op jit(solution)/shard_map/ppermute | solution.py:405
  225.9 39.6 %collective-permute-start.6 = (f32[4,2,16,512]{3,2,1,0:T(8,128)S(1)}, f32[4,2,16,512]{3,2,1,0:T(8,128)S(1)}, u32[]{:S(2)}, u32[]{:S(2)}) collective-permute-start(f32[4,2,16,512]{3,2,1,0:T(8,128)S(1)} %get-tuple-element.46), channel_id=1, source_target_pairs={{0,3},{1,4},{2,5},{3,6},{4,7},{5,0},{6,1},{7,2},{8,11},{9,12},{10,... | collective-permute-start | bytes 786440 | tf_op jit(solution)/shard_map/ppermute | solution.py:405
  237.6 27.9 %collective-permute-start.7 = (f32[4,2,16,512]{3,2,1,0:T(8,128)S(1)}, f32[4,2,16,512]{3,2,1,0:T(8,128)S(1)}, u32[]{:S(2)}, u32[]{:S(2)}) collective-permute-start(f32[4,2,16,512]{3,2,1,0:T(8,128)S(1)} %get-tuple-element.47), channel_id=1, source_target_pairs={{0,4},{1,5},{2,6},{3,7},{4,0},{5,1},{6,2},{7,3},{8,12},{9,13},{10,... | collective-permute-start | bytes 786440 | tf_op jit(solution)/shard_map/ppermute | solution.py:405
  242.5 22.9 %collective-permute-start.8 = (f32[4,2,16,512]{3,2,1,0:T(8,128)S(1)}, f32[4,2,16,512]{3,2,1,0:T(8,128)S(1)}, u32[]{:S(2)}, u32[]{:S(2)}) collective-permute-start(f32[4,2,16,512]{3,2,1,0:T(8,128)S(1)} %get-tuple-element.48), channel_id=1, source_target_pairs={{0,5},{1,6},{2,7},{3,0},{4,1},{5,2},{6,3},{7,4},{8,13},{9,14},{10,... | collective-permute-start | bytes 786440 | tf_op jit(solution)/shard_map/ppermute | solution.py:405
  245.6 19.8 %collective-permute-start.9 = (f32[4,2,16,512]{3,2,1,0:T(8,128)S(1)}, f32[4,2,16,512]{3,2,1,0:T(8,128)S(1)}, u32[]{:S(2)}, u32[]{:S(2)}) collective-permute-start(f32[4,2,16,512]{3,2,1,0:T(8,128)S(1)} %get-tuple-element.49), channel_id=1, source_target_pairs={{0,6},{1,7},{2,0},{3,1},{4,2},{5,3},{6,4},{7,5},{8,14},{9,15},{10,... | collective-permute-start | bytes 786440 | tf_op jit(solution)/shard_map/ppermute | solution.py:405
where the time goes:
time: 268 us; the launch traced here: 267 us
  blocking collectives  167 us (62%)
  Pallas kernels  63.7 us (24%)
  starting transfers between devices  17.9 us (7%)
  waiting for transfers between devices  17 us (6%)
    all_to_all x1, blocking collectives, whole(): lax.all_to_all(planes_first(me, core, field), ALL, 0, 0, tiled=True)  107 us
    all_to_all x2, blocking collectives, summed_pieces(): return jnp.sum(lax.all_to_all(pieces, CHIPS, 0, 0, tiled=True), axis=0)  30.7 us
    all_to_all x2, blocking collectives, gathered_half(): return lax.all_to_all(copies, CHIPS, 0, 0, tiled=True).reshape(-1, 128)  28.9 us
    pallas_call x2, Pallas kernels, basis_rows(): pl.pallas_call(basis_kernel, in_specs=[pl.BlockSpec(memory_space=pltpu.SM...  28.8 us
    ppermute x7, waiting for transfers between devices, whole(): lax.ppermute(blocks[j], 'narrow', [(n, (n + j) % narrow) for n in range(n...  14.1 us
    pallas_call x1, Pallas kernels, planes_first(): pl.pallas_call(planes_kernel, grid=(species // 2, blocks), in_specs=[pl.B...  10.1 us
    ppermute x7, starting transfers between devices, whole(): lax.ppermute(blocks[j], 'narrow', [(n, (n + j) % narrow) for n in range(n...  9.01 us
    pallas_call x1, Pallas kernels, gram_first(): pl.pallas_call(functools.partial(gram_first_kernel, steps), grid=(steps,)...  7.98 us
  transfers between devices with their start and end apart: 11, of which 4 were waited for; matrix products, arithmetic and copies ran while one was open for 0% of the time, Pallas kernels for 8%

commit v1 on v0

--- a/solution.py
+++ b/solution.py
@@ -61,8 +61,8 @@
         in_specs=[pl.BlockSpec(memory_space=pltpu.SMEM)] * 2
         + [pl.BlockSpec((2, ib, points, planes), lambda c, g: (c, g, 0, 0))],
         out_specs=pl.BlockSpec((planes, ib, 2 * points), lambda c, g: (0, c * blocks + g, 0)),
-        out_shape=jax.ShapeDtypeStruct((planes, cells * species // 2, 2 * points), F32),
-        compiler_params=pltpu.CompilerParams(vmem_limit_bytes=60 * MIB),
+        out_shape=pltpu.VMEM((planes, cells * species // 2, 2 * points), F32),
+        compiler_params=pltpu.CompilerParams(vmem_limit_bytes=52 * MIB),
         name="planes_first",
     )(me, core, field)
 
@@ -79,6 +79,20 @@
     half = keep_ref.shape[0]
     keep_ref[...] = packed[pl.ds(pl.multiple_of(core_ref[0] * half, half), half), :]
     send_ref[...] = packed[pl.ds(pl.multiple_of((1 - core_ref[0]) * half, half), half), :]
+
+
+def accumulate(step, main, cross, above, below, mixed):
+    @pl.when(step == 0)
+    def _():
+        main[:256, :256] = above
+        main[256:, :] = below
+        cross[...] = mixed
+
+    @pl.when(step > 0)
+    def _():
+        main[:256, :256] += above
+        main[256:, :] += below
+        cross[...] += mixed
 
 
 def gram_first_kernel(steps, core_ref, y_ref, keep_ref, send_ref, packed, main, cross):
@@ -92,17 +106,9 @@
     ]
     high, low = split2(jnp.concatenate(parts, axis=1))
     mixed = dot16(high, low, NT)
-    full = dot16(high, high, NT)
-
-    @pl.when(step == 0)
-    def _():
-        main[...] = full
-        cross[...] = mixed
-
-    @pl.when(step > 0)
-    def _():
-        main[...] += full
-        cross[...] += mixed
+    above = dot16(high[:256], high[:256], NT)
+    below = dot16(high[256:], high, NT)
+    accumulate(step, main, cross, above, below, mixed)
 
     @pl.when(step == steps - 1)
     def _():
@@ -139,8 +145,11 @@
     )(core, y)
 
 
-def summed_pieces(keep, send, chips):
-    half = keep + lax.ppermute(send, "core", SWAP)
+def paired(keep, send):
+    return keep + lax.ppermute(send, "core", SWAP)
+
+
+def summed_pieces(half, chips):
     pieces = half.reshape(chips, 1, half.shape[0] * 128 // chips)
     return jnp.sum(lax.all_to_all(pieces, CHIPS, 0, 0, tiled=True), axis=0)
 
@@ -234,7 +243,7 @@
     )(start)
 
 
-def basis_kernel(core_ref, mine_ref, other_ref, start_ref, rows_ref, basis_ref, packed, gram):
+def basis_kernel(core_ref, mine_ref, other_ref, start_ref, rows_ref, packed, gram):
     half = mine_ref.shape[0]
     packed[pl.ds(pl.multiple_of(core_ref[0] * half, half), half), :] = mine_ref[...]
     packed[pl.ds(pl.multiple_of((1 - core_ref[0]) * half, half), half), :] = other_ref[...]
@@ -249,9 +258,7 @@
     def sweep(_, rows):
         return orthonormal_rows(dot32(rows, gram[...], NN))
 
-    rows = lax.fori_loop(0, ITERS, sweep, start_ref[...])
-    rows_ref[...] = rows
-    basis_ref[...] = rows.T
+    rows_ref[...] = lax.fori_loop(0, ITERS, sweep, start_ref[...])
 
 
 def basis_rows(core, mine, other, start):
@@ -260,10 +267,7 @@
     return pl.pallas_call(
         basis_kernel,
         in_specs=[pl.BlockSpec(memory_space=pltpu.SMEM), whole, whole, whole],
-        out_shape=(
-            jax.ShapeDtypeStruct((rank, size), F32),
-            jax.ShapeDtypeStruct((size, rank), F32),
-        ),
+        out_shape=jax.ShapeDtypeStruct((rank, size), F32),
         scratch_shapes=[
             pltpu.VMEM((2 * mine.shape[0], 128), F32),
             pltpu.VMEM((size, size), F32),
@@ -271,6 +275,19 @@
         compiler_params=pltpu.CompilerParams(vmem_limit_bytes=16 * MIB),
         name="basis_rows",
     )(core, mine, other, start)
+
+
+def flip_kernel(rows_ref, out_ref):
+    out_ref[...] = rows_ref[...].T
+
+
+def flipped(rows):
+    return pl.pallas_call(
+        flip_kernel,
+        out_shape=jax.ShapeDtypeStruct(rows.shape[::-1], F32),
+        compiler_params=pltpu.CompilerParams(vmem_limit_bytes=4 * MIB),
+        name="flipped",
+    )(rows)
 
 
 def reduce_kernel(me_ref, core_ref, rows_ref, y_ref, *refs):
@@ -297,18 +314,10 @@
             start = pl.multiple_of(rank * s + owner * per, per)
             out_ref[0, s] = reduced[pl.ds(start, per), :]
     high, low = split2(reduced[...])
-    full = dot16(high, high, TN)
     mixed = dot16(high, low, TN)
-
-    @pl.when(step == 0)
-    def _():
-        main[...] = full
-        cross[...] = mixed
-
-    @pl.when(step > 0)
-    def _():
-        main[...] += full
-        cross[...] += mixed
+    above = dot16(high[:, :256], high[:, :256], TN)
+    below = dot16(high[:, 256:], high, TN)
+    accumulate(step, main, cross, above, below, mixed)
 
     @pl.when(step == 3)
     def _():
@@ -396,17 +405,21 @@
     y = planes.reshape(wide, narrow, 2, field.shape[0] // 2, field.shape[1], planes.shape[2])
     rows_first = start_rows(start_first)
     rows_second = start_rows(start_second)
-    own = summed_pieces(*gram_first(core, y), chips)
+    half = paired(*gram_first(core, y))
+    own = summed_pieces(half, chips)
     mine = gathered_half(own, chips)
-    rows_first, basis_first = basis_rows(core, mine, swapped(mine), rows_first)
+    rows_first = basis_rows(core, mine, swapped(mine), rows_first)
     blocks, keep, send = reduce_first(me, core, rows_first, y)
-    own, blocks = lax.optimization_barrier((summed_pieces(keep, send, chips), blocks))
-    moved = [
-        lax.ppermute(blocks[j], "narrow", [(n, (n + j) % narrow) for n in range(narrow)])
-        for j in range(1, narrow)
-    ]
+    half = paired(keep, send)
+    own = summed_pieces(half, chips)
+    moved = []
+    for j in range(1, narrow):
+        ring = [(n, (n + j) % narrow) for n in range(narrow)]
+        moved.append(lax.ppermute(blocks[j], "narrow", ring))
     mine = gathered_half(own, chips)
-    rows_second, basis_second = basis_rows(core, mine, swapped(mine), rows_second)
+    rows_second = basis_rows(core, mine, swapped(mine), rows_second)
+    basis_first = flipped(rows_first)
+    basis_second = flipped(rows_second)
     return (core_blocks(me, rows_second, [blocks[0]] + moved), basis_first, basis_second)
 
 

time: 268 us -> 265 us (0.989)
  Pallas kernels: 63.7 us -> 60.9 us
  transfers between devices with their start and end apart: 11 -> 11, of which waited for: 4 -> 4; matrix products, arithmetic and copies ran while one was open for 0% -> 0% of each run, Pallas kernels for 8% -> 9%
where the time goes in v1:
time: 265 us; the launch traced here: 264 us
  blocking collectives  167 us (63%)
  Pallas kernels  60.9 us (23%)
  starting transfers between devices  17.9 us (7%)
  waiting for transfers between devices  17 us (6%)
    all_to_all x1, blocking collectives, whole(): lax.all_to_all(planes_first(me, core, field), ALL, 0, 0, tiled=True)  107 us
    all_to_all x2, blocking collectives, summed_pieces(): return jnp.sum(lax.all_to_all(pieces, CHIPS, 0, 0, tiled=True), axis=0)  30.7 us
    all_to_all x2, blocking collectives, gathered_half(): return lax.all_to_all(copies, CHIPS, 0, 0, tiled=True).reshape(-1, 128)  28.9 us
    pallas_call x2, Pallas kernels, basis_rows(): pl.pallas_call(basis_kernel, in_specs=[pl.BlockSpec(memory_space=pltpu.SM...  27.1 us
    ppermute x7, waiting for transfers between devices, whole(): moved.append(lax.ppermute(blocks[j], 'narrow', ring))  14.1 us
    ppermute x7, starting transfers between devices, whole(): moved.append(lax.ppermute(blocks[j], 'narrow', ring))  9.01 us
    pallas_call x2, Pallas kernels, start_rows(): pl.pallas_call(start_kernel, out_shape=jax.ShapeDtypeStruct(start.shape[:...  7.71 us
    pallas_call x1, Pallas kernels, planes_first(): pl.pallas_call(planes_kernel, grid=(species // 2, blocks), in_specs=[pl.B...  7.68 us
  transfers between devices with their start and end apart: 11, of which 4 were waited for; matrix products, arithmetic and copies ran while one was open for 0% of the time, Pallas kernels for 9%

profile of v1, /device:TPU:1, one launch (start us, length us, event | category | flops | bytes accessed | tf_op | source)
XLA Modules:
  0.0 264.1 jit_solution(14984385749191313892)
XLA Ops:
  0.6 7.7 %planes_first.1 = f32[256,64,128]{2,1,0:T(8,128)S(1)} custom-call(s32[1]{0:T(128)} %bitcast.me_ref, s32[1]{0:T(128)} %bitcast.1.core_ref, f32[4,32,64,256]{3,2,1,0:T(8,128)} %x_ref.1), custom_call_target="tpu_custom_call" | custom-call | tf_op jit(solution)/shard_map/planes_first/pallas_call | solution.py:58
  8.3 107.1 %all_to_all.25 = f32[256,64,128]{2,1,0:T(8,128)} all-to-all(f32[256,64,128]{2,1,0:T(8,128)S(1)} %planes_first.1), channel_id=1, replica_groups=mesh['board'=8,'core'=2,'narrow'=8] {'board','core','narrow'}, dimensions={0} | all-to-all | bytes 16777216 | tf_op jit(solution)/shard_map/all_to_all | solution.py:404
  115.4 0.0 copy-start
  115.4 7.6 %gram_first.1 = (f32[640,128]{1,0:T(8,128)S(1)}, f32[640,128]{1,0:T(8,128)S(1)}) custom-call(s32[1]{0:T(128)} %bitcast.1.core_ref, f32[16,8,2,2,32,128]{5,4,3,2,1,0:T(8,128)} %bitcast.11), custom_call_target="tpu_custom_call" | custom-call | tf_op jit(solution)/shard_map/gram_first/pallas_call | solution.py:127
  123.0 0.0 copy-start.1
  123.0 2.7 %collective-permute-start = (f32[640,128]{1,0:T(8,128)S(1)}, f32[640,128]{1,0:T(8,128)S(1)}, u32[]{:S(2)}, u32[]{:S(2)}) collective-permute-start(f32[640,128]{1,0:T(8,128)S(1)} %get-tuple-element.16), channel_id=1, source_target_pairs={{0,8},{8,0},{1,9},{9,1},{2,10},{10,2},{3,11},{11,3},{4,12},{12,4},... | collective-permute-start | bytes 983048 | tf_op jit(solution)/shard_map/ppermute | solution.py:149
  125.7 1.3 collective-permute-done
  127.0 15.7 %all_to_all.26 = f32[64,1,1280]{2,1,0:T(1,128)S(1)} all-to-all(f32[64,1,1280]{2,1,0:T(1,128)S(1)} %bitcast.13), channel_id=1, replica_groups=mesh['board'=8,'core'=2,'narrow'=8] {'board','narrow'}, dimensions={0} | all-to-all | bytes 655360 | tf_op jit(solution)/shard_map/all_to_all | solution.py:154
  142.7 0.2 reduce_sum.18
  142.9 0.2 broadcast_in_dim.4
  143.1 14.6 %all_to_all.27 = f32[64,1,1280]{2,1,0:T(1,128)S(1)} all-to-all(f32[64,1,1280]{2,1,0:T(1,128)S(1)} %broadcast_in_dim.4), channel_id=1, replica_groups=mesh['board'=8,'core'=2,'narrow'=8] {'board','narrow'}, dimensions={0} | all-to-all | bytes 655360 | tf_op jit(solution)/shard_map/all_to_all | solution.py:159
  157.6 3.2 %collective-permute-start.1 = (f32[640,128]{1,0:T(8,128)S(1)}, f32[640,128]{1,0:T(8,128)S(1)}, u32[]{:S(2)}, u32[]{:S(2)}) collective-permute-start(f32[640,128]{1,0:T(8,128)S(1)} %bitcast.9), channel_id=1, source_target_pairs={{0,8},{8,0},{1,9},{9,1},{2,10},{10,2},{3,11},{11,3},{4,12},{12,4},... | collective-permute-start | bytes 983048 | tf_op jit(solution)/shard_map/ppermute | solution.py:163
  160.8 0.0 copy-done
  160.8 3.9 %start_rows.2.start_ref = f32[128,512]{1,0:T(8,128)S(1)} custom-call(f32[512,128]{1,0:T(8,128)S(1)} %copy-done), custom_call_target="tpu_custom_call" | custom-call | tf_op jit(solution)/shard_map/start_rows/pallas_call | solution.py:238
  164.7 0.0 collective-permute-done.1.other_ref
  164.7 13.6 %basis_rows.2.rows_ref = f32[128,512]{1,0:T(8,128)S(1)} custom-call(s32[1]{0:T(128)} %bitcast.1.core_ref, f32[640,128]{1,0:T(8,128)S(1)} %bitcast.10, f32[640,128]{1,0:T(8,128)S(1)} %collective-permute-done.1.other_ref, f32[128,512]{1,0:T(8,128)S(1)} %start_rows.2.start_ref), custom_call_target="tpu_custom_call" | custom-call | tf_op jit(solution)/shard_map/basis_rows/pallas_call | solution.py:267
  178.3 7.4 %reduce_first.1 = (f32[4,2,16,512]{3,2,1,0:T(8,128)S(1)}, f32[4,2,16,512]{3,2,1,0:T(8,128)S(1)}, f32[4,2,16,512]{3,2,1,0:T(8,128)S(1)}, f32[4,2,16,512]{3,2,1,0:...) custom-call(s32[1]{0:T(128)} %bitcast.me_ref, ...), custom_call_target="tpu_custom_call" | custom-call | tf_op jit(solution)/shard_map/reduce_first/pallas_call | solution.py:334
  185.7 0.1 collective-permute-start.2
  185.8 1.6 collective-permute-done.2
  187.4 15.1 %all_to_all.28 = f32[64,1,1280]{2,1,0:T(1,128)S(1)} all-to-all(f32[64,1,1280]{2,1,0:T(1,128)S(1)} %bitcast.14), channel_id=1, replica_groups=mesh['board'=8,'core'=2,'narrow'=8] {'board','narrow'}, dimensions={0} | all-to-all | bytes 655360 | tf_op jit(solution)/shard_map/all_to_all | solution.py:154
  202.5 0.2 reduce_sum.19
  202.7 0.2 broadcast_in_dim.5
  202.9 14.4 %all_to_all.29 = f32[64,1,1280]{2,1,0:T(1,128)S(1)} all-to-all(f32[64,1,1280]{2,1,0:T(1,128)S(1)} %broadcast_in_dim.5), channel_id=1, replica_groups=mesh['board'=8,'core'=2,'narrow'=8] {'board','narrow'}, dimensions={0} | all-to-all | bytes 655360 | tf_op jit(solution)/shard_map/all_to_all | solution.py:159
  217.2 2.9 %collective-permute-start.3 = (f32[640,128]{1,0:T(8,128)S(1)}, f32[640,128]{1,0:T(8,128)S(1)}, u32[]{:S(2)}, u32[]{:S(2)}) collective-permute-start(f32[640,128]{1,0:T(8,128)S(1)} %bitcast.7), channel_id=1, source_target_pairs={{0,8},{8,0},{1,9},{9,1},{2,10},{10,2},{3,11},{11,3},{4,12},{12,4},... | collective-permute-start | bytes 983048 | tf_op jit(solution)/shard_map/ppermute | solution.py:163
  220.2 0.7 collective-permute-start.10
  220.9 0.8 collective-permute-start.4
  221.6 0.3 collective-permute-start.5
  221.9 1.4 collective-permute-start.6
  223.3 10.3 %collective-permute-done.10.refs_7_ = f32[4,2,16,512]{3,2,1,0:T(8,128)S(1)} collective-permute-done((f32[4,2,16,512]{3,2,1,0:T(8,128)S(1)}, f32[4,2,16,512]{3,2,1,0:T(8,128)S(1)}, u32[]{:S(2)}, u32[]{:S(2)}) %collective-permute-start.10) | collective-permute-done | bytes 262176 | tf_op jit(solution)/shard_map/ppermute | solution.py:418
  233.6 1.2 collective-permute-start.7
  234.8 3.8 %collective-permute-done.4.refs_1_ = f32[4,2,16,512]{3,2,1,0:T(8,128)S(1)} collective-permute-done((f32[4,2,16,512]{3,2,1,0:T(8,128)S(1)}, f32[4,2,16,512]{3,2,1,0:T(8,128)S(1)}, u32[]{:S(2)}, u32[]{:S(2)}) %collective-permute-start.4) | collective-permute-done | bytes 262176 | tf_op jit(solution)/shard_map/ppermute | solution.py:418
  238.6 3.1 %collective-permute-start.8 = (f32[4,2,16,512]{3,2,1,0:T(8,128)S(1)}, f32[4,2,16,512]{3,2,1,0:T(8,128)S(1)}, u32[]{:S(2)}, u32[]{:S(2)}) collective-permute-start(f32[4,2,16,512]{3,2,1,0:T(8,128)S(1)} %get-tuple-element.24), channel_id=1, source_target_pairs={{0,5},{1,6},{2,7},{3,0},{4,1},{5,2},{6,3},{7,4},{8,13},{9,14},{10,... | collective-permute-start | bytes 786440 | tf_op jit(solution)/shard_map/ppermute | solution.py:418
  241.7 0.0 collective-permute-done.3.other_ref
  241.7 1.6 collective-permute-start.9
  243.2 0.0 copy-done.1
  243.2 3.9 %start_rows.3.start_ref = f32[128,512]{1,0:T(8,128)S(1)} custom-call(f32[512,128]{1,0:T(8,128)S(1)} %copy-done.1), custom_call_target="tpu_custom_call" | custom-call | tf_op jit(solution)/shard_map/start_rows/pallas_call | solution.py:238
  247.1 0.8 flipped.2
  247.9 13.6 %basis_rows.3.rows_ref = f32[128,512]{1,0:T(8,128)S(1)} custom-call(s32[1]{0:T(128)} %bitcast.1.core_ref, f32[640,128]{1,0:T(8,128)S(1)} %bitcast.8, f32[640,128]{1,0:T(8,128)S(1)} %collective-permute-done.3.other_ref, f32[128,512]{1,0:T(8,128)S(1)} %start_rows.3.start_ref), custom_call_target="tpu_custom_call" | custom-call | tf_op jit(solution)/shard_map/basis_rows/pallas_call | solution.py:267
  261.5 0.8 flipped.3
  262.3 0.0 collective-permute-done.5.refs_2_
  262.3 0.0 collective-permute-done.6.refs_3_
  262.4 0.0 collective-permute-done.7.refs_4_
  262.4 0.0 collective-permute-done.8.refs_5_
  262.4 0.0 collective-permute-done.9.refs_6_
  262.4 1.7 core_blocks.1
  (2 shorter events, 0.1 us)
Async XLA Ops:
  115.4 45.4 %copy-start = (f32[512,128]{1,0:T(8,128)S(1)}, f32[512,128]{1,0:T(8,128)}, u32[]{:S(2)}) copy-start(f32[512,128]{1,0:T(8,128)} %start_ref.2) | copy-start | bytes 786436
  123.0 120.2 %copy-start.1 = (f32[512,128]{1,0:T(8,128)S(1)}, f32[512,128]{1,0:T(8,128)}, u32[]{:S(2)}) copy-start(f32[512,128]{1,0:T(8,128)} %start_ref.3) | copy-start | bytes 786436
  123.0 3.9 %collective-permute-start = (f32[640,128]{1,0:T(8,128)S(1)}, f32[640,128]{1,0:T(8,128)S(1)}, u32[]{:S(2)}, u32[]{:S(2)}) collective-permute-start(f32[640,128]{1,0:T(8,128)S(1)} %get-tuple-element.16), channel_id=1, source_target_pairs={{0,8},{8,0},{1,9},{9,1},{2,10},{10,2},{3,11},{11,3},{4,12},{12,4},... | collective-permute-start | bytes 983048 | tf_op jit(solution)/shard_map/ppermute | solution.py:149
  157.6 7.1 %collective-permute-start.1 = (f32[640,128]{1,0:T(8,128)S(1)}, f32[640,128]{1,0:T(8,128)S(1)}, u32[]{:S(2)}, u32[]{:S(2)}) collective-permute-start(f32[640,128]{1,0:T(8,128)S(1)} %bitcast.9), channel_id=1, source_target_pairs={{0,8},{8,0},{1,9},{9,1},{2,10},{10,2},{3,11},{11,3},{4,12},{12,4},... | collective-permute-start | bytes 983048 | tf_op jit(solution)/shard_map/ppermute | solution.py:163
  185.7 1.7 collective-permute-start.2
  217.2 24.4 %collective-permute-start.3 = (f32[640,128]{1,0:T(8,128)S(1)}, f32[640,128]{1,0:T(8,128)S(1)}, u32[]{:S(2)}, u32[]{:S(2)}) collective-permute-start(f32[640,128]{1,0:T(8,128)S(1)} %bitcast.7), channel_id=1, source_target_pairs={{0,8},{8,0},{1,9},{9,1},{2,10},{10,2},{3,11},{11,3},{4,12},{12,4},... | collective-permute-start | bytes 983048 | tf_op jit(solution)/shard_map/ppermute | solution.py:163
  220.2 13.5 %collective-permute-start.10 = (f32[4,2,16,512]{3,2,1,0:T(8,128)S(1)}, f32[4,2,16,512]{3,2,1,0:T(8,128)S(1)}, u32[]{:S(2)}, u32[]{:S(2)}) collective-permute-start(f32[4,2,16,512]{3,2,1,0:T(8,128)S(1)} %get-tuple-element.26), channel_id=1, source_target_pairs={{0,7},{1,0},{2,1},{3,2},{4,3},{5,4},{6,5},{7,6},{8,15},{9,8},{10,9... | collective-permute-start | bytes 786440 | tf_op jit(solution)/shard_map/ppermute | solution.py:418
  220.9 17.7 %collective-permute-start.4 = (f32[4,2,16,512]{3,2,1,0:T(8,128)S(1)}, f32[4,2,16,512]{3,2,1,0:T(8,128)S(1)}, u32[]{:S(2)}, u32[]{:S(2)}) collective-permute-start(f32[4,2,16,512]{3,2,1,0:T(8,128)S(1)} %get-tuple-element.20), channel_id=1, source_target_pairs={{0,1},{1,2},{2,3},{3,4},{4,5},{5,6},{6,7},{7,0},{8,9},{9,10},{10,1... | collective-permute-start | bytes 786440 | tf_op jit(solution)/shard_map/ppermute | solution.py:418
  221.6 40.7 %collective-permute-start.5 = (f32[4,2,16,512]{3,2,1,0:T(8,128)S(1)}, f32[4,2,16,512]{3,2,1,0:T(8,128)S(1)}, u32[]{:S(2)}, u32[]{:S(2)}) collective-permute-start(f32[4,2,16,512]{3,2,1,0:T(8,128)S(1)} %get-tuple-element.21), channel_id=1, source_target_pairs={{0,2},{1,3},{2,4},{3,5},{4,6},{5,7},{6,0},{7,1},{8,10},{9,11},{10,... | collective-permute-start | bytes 786440 | tf_op jit(solution)/shard_map/ppermute | solution.py:418
  221.9 40.4 %collective-permute-start.6 = (f32[4,2,16,512]{3,2,1,0:T(8,128)S(1)}, f32[4,2,16,512]{3,2,1,0:T(8,128)S(1)}, u32[]{:S(2)}, u32[]{:S(2)}) collective-permute-start(f32[4,2,16,512]{3,2,1,0:T(8,128)S(1)} %get-tuple-element.22), channel_id=1, source_target_pairs={{0,3},{1,4},{2,5},{3,6},{4,7},{5,0},{6,1},{7,2},{8,11},{9,12},{10,... | collective-permute-start | bytes 786440 | tf_op jit(solution)/shard_map/ppermute | solution.py:418
  233.6 28.7 %collective-permute-start.7 = (f32[4,2,16,512]{3,2,1,0:T(8,128)S(1)}, f32[4,2,16,512]{3,2,1,0:T(8,128)S(1)}, u32[]{:S(2)}, u32[]{:S(2)}) collective-permute-start(f32[4,2,16,512]{3,2,1,0:T(8,128)S(1)} %get-tuple-element.23), channel_id=1, source_target_pairs={{0,4},{1,5},{2,6},{3,7},{4,0},{5,1},{6,2},{7,3},{8,12},{9,13},{10,... | collective-permute-start | bytes 786440 | tf_op jit(solution)/shard_map/ppermute | solution.py:418
  238.6 23.8 %collective-permute-start.8 = (f32[4,2,16,512]{3,2,1,0:T(8,128)S(1)}, f32[4,2,16,512]{3,2,1,0:T(8,128)S(1)}, u32[]{:S(2)}, u32[]{:S(2)}) collective-permute-start(f32[4,2,16,512]{3,2,1,0:T(8,128)S(1)} %get-tuple-element.24), channel_id=1, source_target_pairs={{0,5},{1,6},{2,7},{3,0},{4,1},{5,2},{6,3},{7,4},{8,13},{9,14},{10,... | collective-permute-start | bytes 786440 | tf_op jit(solution)/shard_map/ppermute | solution.py:418
  241.7 20.7 %collective-permute-start.9 = (f32[4,2,16,512]{3,2,1,0:T(8,128)S(1)}, f32[4,2,16,512]{3,2,1,0:T(8,128)S(1)}, u32[]{:S(2)}, u32[]{:S(2)}) collective-permute-start(f32[4,2,16,512]{3,2,1,0:T(8,128)S(1)} %get-tuple-element.25), channel_id=1, source_target_pairs={{0,6},{1,7},{2,0},{3,1},{4,2},{5,3},{6,4},{7,5},{8,14},{9,15},{10,... | collective-permute-start | bytes 786440 | tf_op jit(solution)/shard_map/ppermute | solution.py:418

commit v2 on v1

--- a/solution.py
+++ b/solution.py
@@ -357,7 +357,12 @@
 
 
 def core_kernel(me_ref, rows_ref, *refs):
-    *block_refs, out_ref = refs
+    *block_refs, out_ref, basis_ref = refs
+
+    @pl.when(pl.program_id(0) == 0)
+    def _():
+        basis_ref[...] = rows_ref[...].T
+
     narrow = len(block_refs)
     taus, lows, per, points = block_refs[0].shape
     rank = rows_ref.shape[0]
@@ -388,8 +393,14 @@
             pl.BlockSpec((rank, points), lambda g: (0, 0)),
         ]
         + [pl.BlockSpec((2, lows, per, points), lambda g: (g, 0, 0, 0))] * narrow,
-        out_specs=pl.BlockSpec((2 * narrow, lows, per, rank), lambda g: (0, g, 0, 0)),
-        out_shape=jax.ShapeDtypeStruct((2 * narrow, groups * lows, per, rank), F32),
+        out_specs=(
+            pl.BlockSpec((2 * narrow, lows, per, rank), lambda g: (0, g, 0, 0)),
+            pl.BlockSpec((points, rank), lambda g: (0, 0)),
+        ),
+        out_shape=(
+            jax.ShapeDtypeStruct((2 * narrow, groups * lows, per, rank), F32),
+            jax.ShapeDtypeStruct((points, rank), F32),
+        ),
         compiler_params=pltpu.CompilerParams(vmem_limit_bytes=12 * MIB),
         name="core_blocks",
     )(me, rows, *blocks)
@@ -419,8 +430,8 @@
     mine = gathered_half(own, chips)
     rows_second = basis_rows(core, mine, swapped(mine), rows_second)
     basis_first = flipped(rows_first)
-    basis_second = flipped(rows_second)
-    return (core_blocks(me, rows_second, [blocks[0]] + moved), basis_first, basis_second)
+    tensor, basis_second = core_blocks(me, rows_second, [blocks[0]] + moved)
+    return (tensor, basis_first, basis_second)
 
 
 def solution(mesh):

time: 265 us -> 264 us (level)
  transfers between devices with their start and end apart: 11 -> 11, of which waited for: 4 -> 4; matrix products, arithmetic and copies ran while one was open for 0% -> 0% of each run, Pallas kernels for 9% -> 8%
where the time goes in v2:
time: 264 us
  blocking collectives  167 us (63%)
  Pallas kernels  60.3 us (23%)
  starting transfers between devices  17.9 us (7%)
  waiting for transfers between devices  17 us (6%)
    all_to_all x1, blocking collectives, whole(): lax.all_to_all(planes_first(me, core, field), ALL, 0, 0, tiled=True)  107 us
    all_to_all x2, blocking collectives, summed_pieces(): return jnp.sum(lax.all_to_all(pieces, CHIPS, 0, 0, tiled=True), axis=0)  30.7 us
    all_to_all x2, blocking collectives, gathered_half(): return lax.all_to_all(copies, CHIPS, 0, 0, tiled=True).reshape(-1, 128)  28.9 us
    pallas_call x2, Pallas kernels, basis_rows(): pl.pallas_call(basis_kernel, in_specs=[pl.BlockSpec(memory_space=pltpu.SM...  27.1 us
    ppermute x7, waiting for transfers between devices, whole(): moved.append(lax.ppermute(blocks[j], 'narrow', ring))  14.1 us
    ppermute x7, starting transfers between devices, whole(): moved.append(lax.ppermute(blocks[j], 'narrow', ring))  9.01 us
    pallas_call x2, Pallas kernels, start_rows(): pl.pallas_call(start_kernel, out_shape=jax.ShapeDtypeStruct(start.shape[:...  7.71 us
    pallas_call x1, Pallas kernels, planes_first(): pl.pallas_call(planes_kernel, grid=(species // 2, blocks), in_specs=[pl.B...  7.68 us
  transfers between devices with their start and end apart: 11, of which 4 were waited for; matrix products, arithmetic and copies ran while one was open for 0% of the time, Pallas kernels for 8%

profile of v2, /device:TPU:1, one launch (start us, length us, event | category | flops | bytes accessed | tf_op | source)
XLA Modules:
  0.0 263.5 jit_solution(9696708419023449508)
XLA Ops:
  0.6 7.7 %planes_first.1 = f32[256,64,128]{2,1,0:T(8,128)S(1)} custom-call(s32[1]{0:T(128)} %bitcast.me_ref, s32[1]{0:T(128)} %bitcast.1.core_ref, f32[4,32,64,256]{3,2,1,0:T(8,128)} %x_ref.1), custom_call_target="tpu_custom_call" | custom-call | tf_op jit(solution)/shard_map/planes_first/pallas_call | solution.py:58
  8.3 107.1 %all_to_all.25 = f32[256,64,128]{2,1,0:T(8,128)} all-to-all(f32[256,64,128]{2,1,0:T(8,128)S(1)} %planes_first.1), channel_id=1, replica_groups=mesh['board'=8,'core'=2,'narrow'=8] {'board','core','narrow'}, dimensions={0} | all-to-all | bytes 16777216 | tf_op jit(solution)/shard_map/all_to_all | solution.py:415
  115.4 0.0 copy-start
  115.4 7.6 %gram_first.1 = (f32[640,128]{1,0:T(8,128)S(1)}, f32[640,128]{1,0:T(8,128)S(1)}) custom-call(s32[1]{0:T(128)} %bitcast.1.core_ref, f32[16,8,2,2,32,128]{5,4,3,2,1,0:T(8,128)} %bitcast.11), custom_call_target="tpu_custom_call" | custom-call | tf_op jit(solution)/shard_map/gram_first/pallas_call | solution.py:127
  123.0 0.0 copy-start.1
  123.0 2.7 %collective-permute-start = (f32[640,128]{1,0:T(8,128)S(1)}, f32[640,128]{1,0:T(8,128)S(1)}, u32[]{:S(2)}, u32[]{:S(2)}) collective-permute-start(f32[640,128]{1,0:T(8,128)S(1)} %get-tuple-element.18), channel_id=1, source_target_pairs={{0,8},{8,0},{1,9},{9,1},{2,10},{10,2},{3,11},{11,3},{4,12},{12,4},... | collective-permute-start | bytes 983048 | tf_op jit(solution)/shard_map/ppermute | solution.py:149
  125.7 1.3 collective-permute-done
  127.0 15.7 %all_to_all.26 = f32[64,1,1280]{2,1,0:T(1,128)S(1)} all-to-all(f32[64,1,1280]{2,1,0:T(1,128)S(1)} %bitcast.13), channel_id=1, replica_groups=mesh['board'=8,'core'=2,'narrow'=8] {'board','narrow'}, dimensions={0} | all-to-all | bytes 655360 | tf_op jit(solution)/shard_map/all_to_all | solution.py:154
  142.7 0.2 reduce_sum.18
  142.9 0.2 broadcast_in_dim.4
  143.1 14.6 %all_to_all.27 = f32[64,1,1280]{2,1,0:T(1,128)S(1)} all-to-all(f32[64,1,1280]{2,1,0:T(1,128)S(1)} %broadcast_in_dim.4), channel_id=1, replica_groups=mesh['board'=8,'core'=2,'narrow'=8] {'board','narrow'}, dimensions={0} | all-to-all | bytes 655360 | tf_op jit(solution)/shard_map/all_to_all | solution.py:159
  157.6 3.2 %collective-permute-start.1 = (f32[640,128]{1,0:T(8,128)S(1)}, f32[640,128]{1,0:T(8,128)S(1)}, u32[]{:S(2)}, u32[]{:S(2)}) collective-permute-start(f32[640,128]{1,0:T(8,128)S(1)} %bitcast.9), channel_id=1, source_target_pairs={{0,8},{8,0},{1,9},{9,1},{2,10},{10,2},{3,11},{11,3},{4,12},{12,4},... | collective-permute-start | bytes 983048 | tf_op jit(solution)/shard_map/ppermute | solution.py:163
  160.8 0.0 copy-done
  160.8 3.9 %start_rows.2.start_ref = f32[128,512]{1,0:T(8,128)S(1)} custom-call(f32[512,128]{1,0:T(8,128)S(1)} %copy-done), custom_call_target="tpu_custom_call" | custom-call | tf_op jit(solution)/shard_map/start_rows/pallas_call | solution.py:238
  164.7 0.0 collective-permute-done.1.other_ref
  164.7 13.6 %basis_rows.2.rows_ref = f32[128,512]{1,0:T(8,128)S(1)} custom-call(s32[1]{0:T(128)} %bitcast.1.core_ref, f32[640,128]{1,0:T(8,128)S(1)} %bitcast.10, f32[640,128]{1,0:T(8,128)S(1)} %collective-permute-done.1.other_ref, f32[128,512]{1,0:T(8,128)S(1)} %start_rows.2.start_ref), custom_call_target="tpu_custom_call" | custom-call | tf_op jit(solution)/shard_map/basis_rows/pallas_call | solution.py:267
  178.3 7.4 %reduce_first.1 = (f32[4,2,16,512]{3,2,1,0:T(8,128)S(1)}, f32[4,2,16,512]{3,2,1,0:T(8,128)S(1)}, f32[4,2,16,512]{3,2,1,0:T(8,128)S(1)}, f32[4,2,16,512]{3,2,1,0:...) custom-call(s32[1]{0:T(128)} %bitcast.me_ref, ...), custom_call_target="tpu_custom_call" | custom-call | tf_op jit(solution)/shard_map/reduce_first/pallas_call | solution.py:334
  185.7 0.1 collective-permute-start.2
  185.8 1.6 collective-permute-done.2
  187.4 15.1 %all_to_all.28 = f32[64,1,1280]{2,1,0:T(1,128)S(1)} all-to-all(f32[64,1,1280]{2,1,0:T(1,128)S(1)} %bitcast.14), channel_id=1, replica_groups=mesh['board'=8,'core'=2,'narrow'=8] {'board','narrow'}, dimensions={0} | all-to-all | bytes 655360 | tf_op jit(solution)/shard_map/all_to_all | solution.py:154
  202.5 0.2 reduce_sum.19
  202.7 0.2 broadcast_in_dim.5
  202.9 14.4 %all_to_all.29 = f32[64,1,1280]{2,1,0:T(1,128)S(1)} all-to-all(f32[64,1,1280]{2,1,0:T(1,128)S(1)} %broadcast_in_dim.5), channel_id=1, replica_groups=mesh['board'=8,'core'=2,'narrow'=8] {'board','narrow'}, dimensions={0} | all-to-all | bytes 655360 | tf_op jit(solution)/shard_map/all_to_all | solution.py:159
  217.2 2.9 %collective-permute-start.3 = (f32[640,128]{1,0:T(8,128)S(1)}, f32[640,128]{1,0:T(8,128)S(1)}, u32[]{:S(2)}, u32[]{:S(2)}) collective-permute-start(f32[640,128]{1,0:T(8,128)S(1)} %bitcast.7), channel_id=1, source_target_pairs={{0,8},{8,0},{1,9},{9,1},{2,10},{10,2},{3,11},{11,3},{4,12},{12,4},... | collective-permute-start | bytes 983048 | tf_op jit(solution)/shard_map/ppermute | solution.py:163
  220.2 0.7 collective-permute-start.10
  220.9 0.8 collective-permute-start.4
  221.6 0.3 collective-permute-start.5
  221.9 1.4 collective-permute-start.6
  223.3 10.3 %collective-permute-done.10.refs_7_ = f32[4,2,16,512]{3,2,1,0:T(8,128)S(1)} collective-permute-done((f32[4,2,16,512]{3,2,1,0:T(8,128)S(1)}, f32[4,2,16,512]{3,2,1,0:T(8,128)S(1)}, u32[]{:S(2)}, u32[]{:S(2)}) %collective-permute-start.10) | collective-permute-done | bytes 262176 | tf_op jit(solution)/shard_map/ppermute | solution.py:429
  233.6 1.2 collective-permute-start.7
  234.8 3.8 %collective-permute-done.4.refs_1_ = f32[4,2,16,512]{3,2,1,0:T(8,128)S(1)} collective-permute-done((f32[4,2,16,512]{3,2,1,0:T(8,128)S(1)}, f32[4,2,16,512]{3,2,1,0:T(8,128)S(1)}, u32[]{:S(2)}, u32[]{:S(2)}) %collective-permute-start.4) | collective-permute-done | bytes 262176 | tf_op jit(solution)/shard_map/ppermute | solution.py:429
  238.6 3.1 %collective-permute-start.8 = (f32[4,2,16,512]{3,2,1,0:T(8,128)S(1)}, f32[4,2,16,512]{3,2,1,0:T(8,128)S(1)}, u32[]{:S(2)}, u32[]{:S(2)}) collective-permute-start(f32[4,2,16,512]{3,2,1,0:T(8,128)S(1)} %get-tuple-element.26), channel_id=1, source_target_pairs={{0,5},{1,6},{2,7},{3,0},{4,1},{5,2},{6,3},{7,4},{8,13},{9,14},{10,... | collective-permute-start | bytes 786440 | tf_op jit(solution)/shard_map/ppermute | solution.py:429
  241.7 0.0 collective-permute-done.3.other_ref
  241.7 1.6 collective-permute-start.9
  243.2 0.0 copy-done.1
  243.2 3.9 %start_rows.3.start_ref = f32[128,512]{1,0:T(8,128)S(1)} custom-call(f32[512,128]{1,0:T(8,128)S(1)} %copy-done.1), custom_call_target="tpu_custom_call" | custom-call | tf_op jit(solution)/shard_map/start_rows/pallas_call | solution.py:238
  247.1 0.8 flipped.1
  247.9 13.6 %basis_rows.3.rows_ref = f32[128,512]{1,0:T(8,128)S(1)} custom-call(s32[1]{0:T(128)} %bitcast.1.core_ref, f32[640,128]{1,0:T(8,128)S(1)} %bitcast.8, f32[640,128]{1,0:T(8,128)S(1)} %collective-permute-done.3.other_ref, f32[128,512]{1,0:T(8,128)S(1)} %start_rows.3.start_ref), custom_call_target="tpu_custom_call" | custom-call | tf_op jit(solution)/shard_map/basis_rows/pallas_call | solution.py:267
  261.5 0.0 collective-permute-done.5.refs_2_
  261.5 0.0 collective-permute-done.6.refs_3_
  261.5 0.0 collective-permute-done.7.refs_4_
  261.5 0.0 collective-permute-done.8.refs_5_
  261.6 0.0 collective-permute-done.9.refs_6_
  261.6 2.0 core_blocks.1
  (2 shorter events, 0.1 us)
Async XLA Ops:
  115.4 45.4 %copy-start = (f32[512,128]{1,0:T(8,128)S(1)}, f32[512,128]{1,0:T(8,128)}, u32[]{:S(2)}) copy-start(f32[512,128]{1,0:T(8,128)} %start_ref.2) | copy-start | bytes 786436
  123.0 120.2 %copy-start.1 = (f32[512,128]{1,0:T(8,128)S(1)}, f32[512,128]{1,0:T(8,128)}, u32[]{:S(2)}) copy-start(f32[512,128]{1,0:T(8,128)} %start_ref.3) | copy-start | bytes 786436
  123.0 3.9 %collective-permute-start = (f32[640,128]{1,0:T(8,128)S(1)}, f32[640,128]{1,0:T(8,128)S(1)}, u32[]{:S(2)}, u32[]{:S(2)}) collective-permute-start(f32[640,128]{1,0:T(8,128)S(1)} %get-tuple-element.18), channel_id=1, source_target_pairs={{0,8},{8,0},{1,9},{9,1},{2,10},{10,2},{3,11},{11,3},{4,12},{12,4},... | collective-permute-start | bytes 983048 | tf_op jit(solution)/shard_map/ppermute | solution.py:149
  157.6 7.1 %collective-permute-start.1 = (f32[640,128]{1,0:T(8,128)S(1)}, f32[640,128]{1,0:T(8,128)S(1)}, u32[]{:S(2)}, u32[]{:S(2)}) collective-permute-start(f32[640,128]{1,0:T(8,128)S(1)} %bitcast.9), channel_id=1, source_target_pairs={{0,8},{8,0},{1,9},{9,1},{2,10},{10,2},{3,11},{11,3},{4,12},{12,4},... | collective-permute-start | bytes 983048 | tf_op jit(solution)/shard_map/ppermute | solution.py:163
  185.7 1.7 collective-permute-start.2
  217.2 24.4 %collective-permute-start.3 = (f32[640,128]{1,0:T(8,128)S(1)}, f32[640,128]{1,0:T(8,128)S(1)}, u32[]{:S(2)}, u32[]{:S(2)}) collective-permute-start(f32[640,128]{1,0:T(8,128)S(1)} %bitcast.7), channel_id=1, source_target_pairs={{0,8},{8,0},{1,9},{9,1},{2,10},{10,2},{3,11},{11,3},{4,12},{12,4},... | collective-permute-start | bytes 983048 | tf_op jit(solution)/shard_map/ppermute | solution.py:163
  220.2 13.5 %collective-permute-start.10 = (f32[4,2,16,512]{3,2,1,0:T(8,128)S(1)}, f32[4,2,16,512]{3,2,1,0:T(8,128)S(1)}, u32[]{:S(2)}, u32[]{:S(2)}) collective-permute-start(f32[4,2,16,512]{3,2,1,0:T(8,128)S(1)} %get-tuple-element.28), channel_id=1, source_target_pairs={{0,7},{1,0},{2,1},{3,2},{4,3},{5,4},{6,5},{7,6},{8,15},{9,8},{10,9... | collective-permute-start | bytes 786440 | tf_op jit(solution)/shard_map/ppermute | solution.py:429
  220.9 17.7 %collective-permute-start.4 = (f32[4,2,16,512]{3,2,1,0:T(8,128)S(1)}, f32[4,2,16,512]{3,2,1,0:T(8,128)S(1)}, u32[]{:S(2)}, u32[]{:S(2)}) collective-permute-start(f32[4,2,16,512]{3,2,1,0:T(8,128)S(1)} %get-tuple-element.22), channel_id=1, source_target_pairs={{0,1},{1,2},{2,3},{3,4},{4,5},{5,6},{6,7},{7,0},{8,9},{9,10},{10,1... | collective-permute-start | bytes 786440 | tf_op jit(solution)/shard_map/ppermute | solution.py:429
  221.6 39.9 %collective-permute-start.5 = (f32[4,2,16,512]{3,2,1,0:T(8,128)S(1)}, f32[4,2,16,512]{3,2,1,0:T(8,128)S(1)}, u32[]{:S(2)}, u32[]{:S(2)}) collective-permute-start(f32[4,2,16,512]{3,2,1,0:T(8,128)S(1)} %get-tuple-element.23), channel_id=1, source_target_pairs={{0,2},{1,3},{2,4},{3,5},{4,6},{5,7},{6,0},{7,1},{8,10},{9,11},{10,... | collective-permute-start | bytes 786440 | tf_op jit(solution)/shard_map/ppermute | solution.py:429
  221.9 39.6 %collective-permute-start.6 = (f32[4,2,16,512]{3,2,1,0:T(8,128)S(1)}, f32[4,2,16,512]{3,2,1,0:T(8,128)S(1)}, u32[]{:S(2)}, u32[]{:S(2)}) collective-permute-start(f32[4,2,16,512]{3,2,1,0:T(8,128)S(1)} %get-tuple-element.24), channel_id=1, source_target_pairs={{0,3},{1,4},{2,5},{3,6},{4,7},{5,0},{6,1},{7,2},{8,11},{9,12},{10,... | collective-permute-start | bytes 786440 | tf_op jit(solution)/shard_map/ppermute | solution.py:429
  233.6 27.9 %collective-permute-start.7 = (f32[4,2,16,512]{3,2,1,0:T(8,128)S(1)}, f32[4,2,16,512]{3,2,1,0:T(8,128)S(1)}, u32[]{:S(2)}, u32[]{:S(2)}) collective-permute-start(f32[4,2,16,512]{3,2,1,0:T(8,128)S(1)} %get-tuple-element.25), channel_id=1, source_target_pairs={{0,4},{1,5},{2,6},{3,7},{4,0},{5,1},{6,2},{7,3},{8,12},{9,13},{10,... | collective-permute-start | bytes 786440 | tf_op jit(solution)/shard_map/ppermute | solution.py:429
  238.6 23.0 %collective-permute-start.8 = (f32[4,2,16,512]{3,2,1,0:T(8,128)S(1)}, f32[4,2,16,512]{3,2,1,0:T(8,128)S(1)}, u32[]{:S(2)}, u32[]{:S(2)}) collective-permute-start(f32[4,2,16,512]{3,2,1,0:T(8,128)S(1)} %get-tuple-element.26), channel_id=1, source_target_pairs={{0,5},{1,6},{2,7},{3,0},{4,1},{5,2},{6,3},{7,4},{8,13},{9,14},{10,... | collective-permute-start | bytes 786440 | tf_op jit(solution)/shard_map/ppermute | solution.py:429
  241.7 19.9 %collective-permute-start.9 = (f32[4,2,16,512]{3,2,1,0:T(8,128)S(1)}, f32[4,2,16,512]{3,2,1,0:T(8,128)S(1)}, u32[]{:S(2)}, u32[]{:S(2)}) collective-permute-start(f32[4,2,16,512]{3,2,1,0:T(8,128)S(1)} %get-tuple-element.27), channel_id=1, source_target_pairs={{0,6},{1,7},{2,0},{3,1},{4,2},{5,3},{6,4},{7,5},{8,14},{9,15},{10,... | collective-permute-start | bytes 786440 | tf_op jit(solution)/shard_map/ppermute | solution.py:429

commit v3 on v2

--- a/solution.py
+++ b/solution.py
@@ -45,10 +45,12 @@
 def planes_kernel(me_ref, core_ref, x_ref, out_ref):
     ib = x_ref.shape[1]
     rows = x_ref.shape[3]
-    flat = out_ref.reshape(rows * ib, out_ref.shape[2])
+    every = out_ref.shape[1]
+    flat = out_ref.reshape(rows * every, out_ref.shape[2])
+    base = (pl.program_id(0) * pl.num_programs(1) + pl.program_id(1)) * ib
     for i in range(ib):
         pair = jnp.concatenate([x_ref[0, i], x_ref[1, i]], axis=0)
-        flat[pl.ds(i, rows, stride=ib), :] = pair.T
+        flat[pl.ds(base + i, rows, stride=every), :] = pair.T
 
 
 def planes_first(me, core, field):
@@ -60,7 +62,7 @@
         grid=(species // 2, blocks),
         in_specs=[pl.BlockSpec(memory_space=pltpu.SMEM)] * 2
         + [pl.BlockSpec((2, ib, points, planes), lambda c, g: (c, g, 0, 0))],
-        out_specs=pl.BlockSpec((planes, ib, 2 * points), lambda c, g: (0, c * blocks + g, 0)),
+        out_specs=pl.BlockSpec(memory_space=pltpu.VMEM),
         out_shape=pltpu.VMEM((planes, cells * species // 2, 2 * points), F32),
         compiler_params=pltpu.CompilerParams(vmem_limit_bytes=52 * MIB),
         name="planes_first",

time: 264 us -> 267 us (1.011)
  Pallas kernels: 60.3 us -> 63.4 us
    pallas_call x1, Pallas kernels: 7.68 us -> 10.8 us  [planes_first(): pl.pallas_call(planes_kernel, grid=(species // 2, blocks), in_specs=[pl.B...]
where the time goes in v3:
time: 267 us
  blocking collectives  167 us (63%)
  Pallas kernels  63.4 us (24%)
  starting transfers between devices  17.9 us (7%)
  waiting for transfers between devices  17 us (6%)
    all_to_all x1, blocking collectives, whole(): lax.all_to_all(planes_first(me, core, field), ALL, 0, 0, tiled=True)  107 us
    all_to_all x2, blocking collectives, summed_pieces(): return jnp.sum(lax.all_to_all(pieces, CHIPS, 0, 0, tiled=True), axis=0)  30.8 us
    all_to_all x2, blocking collectives, gathered_half(): return lax.all_to_all(copies, CHIPS, 0, 0, tiled=True).reshape(-1, 128)  28.9 us
    pallas_call x2, Pallas kernels, basis_rows(): pl.pallas_call(basis_kernel, in_specs=[pl.BlockSpec(memory_space=pltpu.SM...  27.1 us
    ppermute x7, waiting for transfers between devices, whole(): moved.append(lax.ppermute(blocks[j], 'narrow', ring))  14.1 us
    pallas_call x1, Pallas kernels, planes_first(): pl.pallas_call(planes_kernel, grid=(species // 2, blocks), in_specs=[pl.B...  10.8 us
    ppermute x7, starting transfers between devices, whole(): moved.append(lax.ppermute(blocks[j], 'narrow', ring))  9.01 us
    pallas_call x2, Pallas kernels, start_rows(): pl.pallas_call(start_kernel, out_shape=jax.ShapeDtypeStruct(start.shape[:...  7.71 us
  transfers between devices with their start and end apart: 11, of which 4 were waited for; matrix products, arithmetic and copies ran while one was open for 0% of the time, Pallas kernels for 8%

profile of v3, /device:TPU:1, one launch (start us, length us, event | category | flops | bytes accessed | tf_op | source)
XLA Modules:
  0.0 266.6 jit_solution(5363679181442802886)
XLA Ops:
  0.6 10.8 %planes_first.1 = f32[256,64,128]{2,1,0:T(8,128)S(1)} custom-call(s32[1]{0:T(128)} %bitcast.me_ref, s32[1]{0:T(128)} %bitcast.1.core_ref, f32[4,32,64,256]{3,2,1,0:T(8,128)} %x_ref.1), custom_call_target="tpu_custom_call" | custom-call | tf_op jit(solution)/shard_map/planes_first/pallas_call | solution.py:60
  11.4 107.1 %all_to_all.25 = f32[256,64,128]{2,1,0:T(8,128)} all-to-all(f32[256,64,128]{2,1,0:T(8,128)S(1)} %planes_first.1), channel_id=1, replica_groups=mesh['board'=8,'core'=2,'narrow'=8] {'board','core','narrow'}, dimensions={0} | all-to-all | bytes 16777216 | tf_op jit(solution)/shard_map/all_to_all | solution.py:417
  118.5 0.0 copy-start
  118.5 7.6 %gram_first.1 = (f32[640,128]{1,0:T(8,128)S(1)}, f32[640,128]{1,0:T(8,128)S(1)}) custom-call(s32[1]{0:T(128)} %bitcast.1.core_ref, f32[16,8,2,2,32,128]{5,4,3,2,1,0:T(8,128)} %bitcast.11), custom_call_target="tpu_custom_call" | custom-call | tf_op jit(solution)/shard_map/gram_first/pallas_call | solution.py:129
  126.1 0.0 copy-start.1
  126.1 2.7 %collective-permute-start = (f32[640,128]{1,0:T(8,128)S(1)}, f32[640,128]{1,0:T(8,128)S(1)}, u32[]{:S(2)}, u32[]{:S(2)}) collective-permute-start(f32[640,128]{1,0:T(8,128)S(1)} %get-tuple-element.18), channel_id=1, source_target_pairs={{0,8},{8,0},{1,9},{9,1},{2,10},{10,2},{3,11},{11,3},{4,12},{12,4},... | collective-permute-start | bytes 983048 | tf_op jit(solution)/shard_map/ppermute | solution.py:151
  128.8 1.3 collective-permute-done
  130.1 15.7 %all_to_all.26 = f32[64,1,1280]{2,1,0:T(1,128)S(1)} all-to-all(f32[64,1,1280]{2,1,0:T(1,128)S(1)} %bitcast.13), channel_id=1, replica_groups=mesh['board'=8,'core'=2,'narrow'=8] {'board','narrow'}, dimensions={0} | all-to-all | bytes 655360 | tf_op jit(solution)/shard_map/all_to_all | solution.py:156
  145.8 0.2 reduce_sum.18
  146.0 0.2 broadcast_in_dim.4
  146.2 14.6 %all_to_all.27 = f32[64,1,1280]{2,1,0:T(1,128)S(1)} all-to-all(f32[64,1,1280]{2,1,0:T(1,128)S(1)} %broadcast_in_dim.4), channel_id=1, replica_groups=mesh['board'=8,'core'=2,'narrow'=8] {'board','narrow'}, dimensions={0} | all-to-all | bytes 655360 | tf_op jit(solution)/shard_map/all_to_all | solution.py:161
  160.7 3.2 %collective-permute-start.1 = (f32[640,128]{1,0:T(8,128)S(1)}, f32[640,128]{1,0:T(8,128)S(1)}, u32[]{:S(2)}, u32[]{:S(2)}) collective-permute-start(f32[640,128]{1,0:T(8,128)S(1)} %bitcast.9), channel_id=1, source_target_pairs={{0,8},{8,0},{1,9},{9,1},{2,10},{10,2},{3,11},{11,3},{4,12},{12,4},... | collective-permute-start | bytes 983048 | tf_op jit(solution)/shard_map/ppermute | solution.py:165
  163.9 0.0 copy-done
  163.9 3.9 %start_rows.2.start_ref = f32[128,512]{1,0:T(8,128)S(1)} custom-call(f32[512,128]{1,0:T(8,128)S(1)} %copy-done), custom_call_target="tpu_custom_call" | custom-call | tf_op jit(solution)/shard_map/start_rows/pallas_call | solution.py:240
  167.8 0.0 collective-permute-done.1.other_ref
  167.8 13.6 %basis_rows.2.rows_ref = f32[128,512]{1,0:T(8,128)S(1)} custom-call(s32[1]{0:T(128)} %bitcast.1.core_ref, f32[640,128]{1,0:T(8,128)S(1)} %bitcast.10, f32[640,128]{1,0:T(8,128)S(1)} %collective-permute-done.1.other_ref, f32[128,512]{1,0:T(8,128)S(1)} %start_rows.2.start_ref), custom_call_target="tpu_custom_call" | custom-call | tf_op jit(solution)/shard_map/basis_rows/pallas_call | solution.py:269
  181.4 7.4 %reduce_first.1 = (f32[4,2,16,512]{3,2,1,0:T(8,128)S(1)}, f32[4,2,16,512]{3,2,1,0:T(8,128)S(1)}, f32[4,2,16,512]{3,2,1,0:T(8,128)S(1)}, f32[4,2,16,512]{3,2,1,0:...) custom-call(s32[1]{0:T(128)} %bitcast.me_ref, ...), custom_call_target="tpu_custom_call" | custom-call | tf_op jit(solution)/shard_map/reduce_first/pallas_call | solution.py:336
  188.8 0.1 collective-permute-start.2
  188.9 1.6 collective-permute-done.2
  190.5 15.1 %all_to_all.28 = f32[64,1,1280]{2,1,0:T(1,128)S(1)} all-to-all(f32[64,1,1280]{2,1,0:T(1,128)S(1)} %bitcast.14), channel_id=1, replica_groups=mesh['board'=8,'core'=2,'narrow'=8] {'board','narrow'}, dimensions={0} | all-to-all | bytes 655360 | tf_op jit(solution)/shard_map/all_to_all | solution.py:156
  205.6 0.2 reduce_sum.19
  205.8 0.2 broadcast_in_dim.5
  206.0 14.4 %all_to_all.29 = f32[64,1,1280]{2,1,0:T(1,128)S(1)} all-to-all(f32[64,1,1280]{2,1,0:T(1,128)S(1)} %broadcast_in_dim.5), channel_id=1, replica_groups=mesh['board'=8,'core'=2,'narrow'=8] {'board','narrow'}, dimensions={0} | all-to-all | bytes 655360 | tf_op jit(solution)/shard_map/all_to_all | solution.py:161
  220.4 2.9 %collective-permute-start.3 = (f32[640,128]{1,0:T(8,128)S(1)}, f32[640,128]{1,0:T(8,128)S(1)}, u32[]{:S(2)}, u32[]{:S(2)}) collective-permute-start(f32[640,128]{1,0:T(8,128)S(1)} %bitcast.7), channel_id=1, source_target_pairs={{0,8},{8,0},{1,9},{9,1},{2,10},{10,2},{3,11},{11,3},{4,12},{12,4},... | collective-permute-start | bytes 983048 | tf_op jit(solution)/shard_map/ppermute | solution.py:165
  223.3 0.7 collective-permute-start.10
  224.0 0.8 collective-permute-start.4
  224.7 0.3 collective-permute-start.5
  225.0 1.4 collective-permute-start.6
  226.4 10.3 %collective-permute-done.10.refs_7_ = f32[4,2,16,512]{3,2,1,0:T(8,128)S(1)} collective-permute-done((f32[4,2,16,512]{3,2,1,0:T(8,128)S(1)}, f32[4,2,16,512]{3,2,1,0:T(8,128)S(1)}, u32[]{:S(2)}, u32[]{:S(2)}) %collective-permute-start.10) | collective-permute-done | bytes 262176 | tf_op jit(solution)/shard_map/ppermute | solution.py:431
  236.7 1.2 collective-permute-start.7
  237.9 3.8 %collective-permute-done.4.refs_1_ = f32[4,2,16,512]{3,2,1,0:T(8,128)S(1)} collective-permute-done((f32[4,2,16,512]{3,2,1,0:T(8,128)S(1)}, f32[4,2,16,512]{3,2,1,0:T(8,128)S(1)}, u32[]{:S(2)}, u32[]{:S(2)}) %collective-permute-start.4) | collective-permute-done | bytes 262176 | tf_op jit(solution)/shard_map/ppermute | solution.py:431
  241.7 3.1 %collective-permute-start.8 = (f32[4,2,16,512]{3,2,1,0:T(8,128)S(1)}, f32[4,2,16,512]{3,2,1,0:T(8,128)S(1)}, u32[]{:S(2)}, u32[]{:S(2)}) collective-permute-start(f32[4,2,16,512]{3,2,1,0:T(8,128)S(1)} %get-tuple-element.26), channel_id=1, source_target_pairs={{0,5},{1,6},{2,7},{3,0},{4,1},{5,2},{6,3},{7,4},{8,13},{9,14},{10,... | collective-permute-start | bytes 786440 | tf_op jit(solution)/shard_map/ppermute | solution.py:431
  244.8 0.0 collective-permute-done.3.other_ref
  244.8 1.6 collective-permute-start.9
  246.4 0.0 copy-done.1
  246.4 3.9 %start_rows.3.start_ref = f32[128,512]{1,0:T(8,128)S(1)} custom-call(f32[512,128]{1,0:T(8,128)S(1)} %copy-done.1), custom_call_target="tpu_custom_call" | custom-call | tf_op jit(solution)/shard_map/start_rows/pallas_call | solution.py:240
  250.2 0.8 flipped.1
  251.1 13.6 %basis_rows.3.rows_ref = f32[128,512]{1,0:T(8,128)S(1)} custom-call(s32[1]{0:T(128)} %bitcast.1.core_ref, f32[640,128]{1,0:T(8,128)S(1)} %bitcast.8, f32[640,128]{1,0:T(8,128)S(1)} %collective-permute-done.3.other_ref, f32[128,512]{1,0:T(8,128)S(1)} %start_rows.3.start_ref), custom_call_target="tpu_custom_call" | custom-call | tf_op jit(solution)/shard_map/basis_rows/pallas_call | solution.py:269
  264.6 0.0 collective-permute-done.5.refs_2_
  264.6 0.0 collective-permute-done.6.refs_3_
  264.6 0.0 collective-permute-done.7.refs_4_
  264.6 0.0 collective-permute-done.8.refs_5_
  264.7 0.0 collective-permute-done.9.refs_6_
  264.7 2.0 core_blocks.1
  (2 shorter events, 0.1 us)
Async XLA Ops:
  118.5 45.4 %copy-start = (f32[512,128]{1,0:T(8,128)S(1)}, f32[512,128]{1,0:T(8,128)}, u32[]{:S(2)}) copy-start(f32[512,128]{1,0:T(8,128)} %start_ref.2) | copy-start | bytes 786436
  126.1 120.3 %copy-start.1 = (f32[512,128]{1,0:T(8,128)S(1)}, f32[512,128]{1,0:T(8,128)}, u32[]{:S(2)}) copy-start(f32[512,128]{1,0:T(8,128)} %start_ref.3) | copy-start | bytes 786436
  126.1 3.9 %collective-permute-start = (f32[640,128]{1,0:T(8,128)S(1)}, f32[640,128]{1,0:T(8,128)S(1)}, u32[]{:S(2)}, u32[]{:S(2)}) collective-permute-start(f32[640,128]{1,0:T(8,128)S(1)} %get-tuple-element.18), channel_id=1, source_target_pairs={{0,8},{8,0},{1,9},{9,1},{2,10},{10,2},{3,11},{11,3},{4,12},{12,4},... | collective-permute-start | bytes 983048 | tf_op jit(solution)/shard_map/ppermute | solution.py:151
  160.7 7.1 %collective-permute-start.1 = (f32[640,128]{1,0:T(8,128)S(1)}, f32[640,128]{1,0:T(8,128)S(1)}, u32[]{:S(2)}, u32[]{:S(2)}) collective-permute-start(f32[640,128]{1,0:T(8,128)S(1)} %bitcast.9), channel_id=1, source_target_pairs={{0,8},{8,0},{1,9},{9,1},{2,10},{10,2},{3,11},{11,3},{4,12},{12,4},... | collective-permute-start | bytes 983048 | tf_op jit(solution)/shard_map/ppermute | solution.py:165
  188.8 1.7 collective-permute-start.2
  220.4 24.4 %collective-permute-start.3 = (f32[640,128]{1,0:T(8,128)S(1)}, f32[640,128]{1,0:T(8,128)S(1)}, u32[]{:S(2)}, u32[]{:S(2)}) collective-permute-start(f32[640,128]{1,0:T(8,128)S(1)} %bitcast.7), channel_id=1, source_target_pairs={{0,8},{8,0},{1,9},{9,1},{2,10},{10,2},{3,11},{11,3},{4,12},{12,4},... | collective-permute-start | bytes 983048 | tf_op jit(solution)/shard_map/ppermute | solution.py:165
  223.3 13.5 %collective-permute-start.10 = (f32[4,2,16,512]{3,2,1,0:T(8,128)S(1)}, f32[4,2,16,512]{3,2,1,0:T(8,128)S(1)}, u32[]{:S(2)}, u32[]{:S(2)}) collective-permute-start(f32[4,2,16,512]{3,2,1,0:T(8,128)S(1)} %get-tuple-element.28), channel_id=1, source_target_pairs={{0,7},{1,0},{2,1},{3,2},{4,3},{5,4},{6,5},{7,6},{8,15},{9,8},{10,9... | collective-permute-start | bytes 786440 | tf_op jit(solution)/shard_map/ppermute | solution.py:431
  224.0 17.7 %collective-permute-start.4 = (f32[4,2,16,512]{3,2,1,0:T(8,128)S(1)}, f32[4,2,16,512]{3,2,1,0:T(8,128)S(1)}, u32[]{:S(2)}, u32[]{:S(2)}) collective-permute-start(f32[4,2,16,512]{3,2,1,0:T(8,128)S(1)} %get-tuple-element.22), channel_id=1, source_target_pairs={{0,1},{1,2},{2,3},{3,4},{4,5},{5,6},{6,7},{7,0},{8,9},{9,10},{10,1... | collective-permute-start | bytes 786440 | tf_op jit(solution)/shard_map/ppermute | solution.py:431
  224.7 39.9 %collective-permute-start.5 = (f32[4,2,16,512]{3,2,1,0:T(8,128)S(1)}, f32[4,2,16,512]{3,2,1,0:T(8,128)S(1)}, u32[]{:S(2)}, u32[]{:S(2)}) collective-permute-start(f32[4,2,16,512]{3,2,1,0:T(8,128)S(1)} %get-tuple-element.23), channel_id=1, source_target_pairs={{0,2},{1,3},{2,4},{3,5},{4,6},{5,7},{6,0},{7,1},{8,10},{9,11},{10,... | collective-permute-start | bytes 786440 | tf_op jit(solution)/shard_map/ppermute | solution.py:431
  225.0 39.6 %collective-permute-start.6 = (f32[4,2,16,512]{3,2,1,0:T(8,128)S(1)}, f32[4,2,16,512]{3,2,1,0:T(8,128)S(1)}, u32[]{:S(2)}, u32[]{:S(2)}) collective-permute-start(f32[4,2,16,512]{3,2,1,0:T(8,128)S(1)} %get-tuple-element.24), channel_id=1, source_target_pairs={{0,3},{1,4},{2,5},{3,6},{4,7},{5,0},{6,1},{7,2},{8,11},{9,12},{10,... | collective-permute-start | bytes 786440 | tf_op jit(solution)/shard_map/ppermute | solution.py:431
  236.7 27.9 %collective-permute-start.7 = (f32[4,2,16,512]{3,2,1,0:T(8,128)S(1)}, f32[4,2,16,512]{3,2,1,0:T(8,128)S(1)}, u32[]{:S(2)}, u32[]{:S(2)}) collective-permute-start(f32[4,2,16,512]{3,2,1,0:T(8,128)S(1)} %get-tuple-element.25), channel_id=1, source_target_pairs={{0,4},{1,5},{2,6},{3,7},{4,0},{5,1},{6,2},{7,3},{8,12},{9,13},{10,... | collective-permute-start | bytes 786440 | tf_op jit(solution)/shard_map/ppermute | solution.py:431
  241.7 23.0 %collective-permute-start.8 = (f32[4,2,16,512]{3,2,1,0:T(8,128)S(1)}, f32[4,2,16,512]{3,2,1,0:T(8,128)S(1)}, u32[]{:S(2)}, u32[]{:S(2)}) collective-permute-start(f32[4,2,16,512]{3,2,1,0:T(8,128)S(1)} %get-tuple-element.26), channel_id=1, source_target_pairs={{0,5},{1,6},{2,7},{3,0},{4,1},{5,2},{6,3},{7,4},{8,13},{9,14},{10,... | collective-permute-start | bytes 786440 | tf_op jit(solution)/shard_map/ppermute | solution.py:431
  244.8 19.9 %collective-permute-start.9 = (f32[4,2,16,512]{3,2,1,0:T(8,128)S(1)}, f32[4,2,16,512]{3,2,1,0:T(8,128)S(1)}, u32[]{:S(2)}, u32[]{:S(2)}) collective-permute-start(f32[4,2,16,512]{3,2,1,0:T(8,128)S(1)} %get-tuple-element.27), channel_id=1, source_target_pairs={{0,6},{1,7},{2,0},{3,1},{4,2},{5,3},{6,4},{7,5},{8,14},{9,15},{10,... | collective-permute-start | bytes 786440 | tf_op jit(solution)/shard_map/ppermute | solution.py:431
